TPU v7x, 256 devices: a whole 4x4x8 slice. The times are simulated.
256 devices in a mesh: blk: 64 (over z, x, y_hi), slab: 4 (over y_lo, core).
Axes of the slice: x: 4, y: 4 (y_hi: 2, y_lo: 2; y = y_hi * 2 + y_lo), z: 8, core: 2. Of those that a mesh axis runs over, the one named last changes fastest.
Arguments:
- a_tiles: bfloat16 [32768, 8192], P('blk', 'slab'), may hold values from -0.125 to 0.125
- tile_cols: int32 [128, 4, 8], P('blk', 'slab'), may hold values from 0 to 15, as said below
- tile_counts: int32 [128, 4], P('blk', 'slab'), may hold values from 1 to 8, as said below
- scaling: float32 [16384], P('slab'), may hold values from 0.1 to 10
- panel: int32 [1], replicated, may hold values from 0 to 127
Outputs:
- normal_band: float32 [32768, 3, 512], P('blk', None, 'slab')
Inputs may be any that keep to these rules, and one draw needn't show every extreme that they name: `tile_cols`: the 8 column tiles listed for one row block in one slab are distinct. `tile_counts`: the largest count is 8 in every draw.
All inputs are finite; a program needn't handle non-finite values.
Results may differ from a plain program's by a relative error of at most 0.0015.
Values may be sent and summed in bfloat16 or wider, within the bound.
No kernel may reach another device: no remote copies, remote signals or barrier semaphores. Data moves between devices by JAX's collectives and lax.ppermute only.
A program may use at most 64 MiB of HBM per device.

v0:
```python
import jax
import jax.numpy as jnp
from jax import lax
from jax.sharding import PartitionSpec as P

ridge_shift = 0.05


def from_behind(value, axis, by):
    peers = lax.axis_size(axis)
    return lax.ppermute(value, axis, [(i, (i + by) % peers) for i in range(peers)])


def body(a_tiles, tile_cols, tile_counts, scaling, panel):
    group_rows = a_tiles.shape[0]
    blocks_here = tile_cols.shape[0]
    slot_count = tile_cols.shape[2]
    tile_size = group_rows // blocks_here
    col_tiles = scaling.shape[0] // tile_size
    slab_count = lax.axis_size("slab")
    group_pos = lax.axis_index("blk")
    slab_pos = lax.axis_index("slab")
    local_width = group_rows // slab_count
    own_cols = tile_cols[:, 0, :]
    own_counts = tile_counts[:, 0]
    slot_ids = jnp.arange(slot_count, dtype=jnp.int32)
    live = slot_ids[None, :] < own_counts[:, None]
    picked = scaling.reshape(col_tiles, tile_size)[own_cols]
    picked = jnp.where(live[..., None], picked, jnp.float32(0.0))
    own_tiles = a_tiles.reshape(blocks_here, tile_size, slot_count, tile_size)
    scaled = (own_tiles.astype(jnp.float32) * picked[:, None]).astype(jnp.bfloat16)
    flat_scaled = scaled.reshape(blocks_here, tile_size, slot_count * tile_size)

    def visit_group(tile_data, col_list, count_list):
        matches = (col_list[:, 0, :, None] == jnp.arange(col_tiles, dtype=jnp.int32)) & (
            slot_ids[None, :] < count_list[:, 0][:, None]
        )[..., None]
        found = jnp.any(matches, axis=1).astype(jnp.int32)
        lookup = jnp.sum(jnp.where(matches, slot_ids[None, :, None], 0), axis=1) + slot_count * (
            1 - found
        )
        slot_index = lookup[:, own_cols.reshape(-1)]
        visiting = tile_data.reshape(blocks_here, tile_size, slot_count, tile_size)
        padded = jnp.concatenate(
            [visiting, jnp.zeros((blocks_here, tile_size, 1, tile_size), jnp.bfloat16)], axis=2
        )
        columns = []
        for other_block in range(blocks_here):
            gathered = jnp.take(padded[other_block], slot_index[other_block], axis=1)
            gathered = gathered.reshape(tile_size, blocks_here, slot_count * tile_size)
            product = jnp.einsum(
                "axk,zak->axz", flat_scaled, gathered, preferred_element_type=jnp.float32
            )
            columns.append(product.reshape(group_rows, tile_size))
        return jnp.concatenate(columns, axis=1)

    payload = (a_tiles, tile_cols, tile_counts)
    planes = [visit_group(a_tiles, tile_cols, tile_counts)]
    moving = payload
    for repeat in range(2):
        moving = from_behind((moving[0], moving[1], moving[2]), "blk", 1)
        planes.append(visit_group(moving[0], moving[1], moving[2]))
    partial_band = jnp.stack(planes, axis=1)
    normal_rows = lax.psum_scatter(partial_band, "slab", scatter_dimension=2, tiled=True)
    row_ids = jnp.arange(group_rows, dtype=jnp.int32)
    col_ids = slab_pos * local_width + jnp.arange(local_width, dtype=jnp.int32)
    ridge_add = jnp.where(
        row_ids[:, None] == col_ids[None, :], jnp.float32(ridge_shift), jnp.float32(0.0)
    )
    plane_zero = normal_rows[:, 0, :] + ridge_add
    plane_one = normal_rows[:, 1, :]
    plane_two = normal_rows[:, 2, :]
    pivot_block = panel[0]
    pivot_group = pivot_block // blocks_here
    pivot_pos = pivot_block % blocks_here
    holds_column = group_pos == pivot_group
    panel_cols = (
        pivot_pos * tile_size + jnp.arange(tile_size, dtype=jnp.int32) - slab_pos * local_width
    )
    panel_inside = (panel_cols >= 0) & (panel_cols < local_width)
    taken = jnp.take(plane_zero, jnp.clip(panel_cols, 0, local_width - 1), axis=1)
    panel_piece = jnp.where(holds_column & panel_inside[None, :], taken, jnp.float32(0.0))
    panel_column = lax.psum(panel_piece, "slab")
    pivot_tile = lax.dynamic_slice(
        panel_column, (pivot_pos * tile_size, jnp.int32(0)), (tile_size, tile_size)
    )
    identity = jnp.eye(tile_size, dtype=jnp.float32)
    pivot_tile = jnp.where(holds_column, pivot_tile, identity)
    factor = jnp.linalg.cholesky(pivot_tile)
    solved_own = jax.scipy.linalg.solve_triangular(factor, panel_column.T, lower=True).T
    row_blocks = row_ids // tile_size
    is_pivot = row_blocks == pivot_pos
    mask_own = holds_column & jnp.logical_not(is_pivot)
    lower_own = jnp.where(mask_own[:, None], solved_own, jnp.float32(0.0))
    plane_zero = plane_zero - jnp.dot(
        lower_own,
        lower_own[col_ids].T,
        precision=lax.Precision.HIGHEST,
        preferred_element_type=jnp.float32,
    )
    stacked_factor = jnp.tile(factor, (blocks_here, 1))
    new_column = jnp.where(is_pivot[:, None], stacked_factor, solved_own)
    within_panel = col_ids - pivot_pos * tile_size
    column_ok = (within_panel >= 0) & (within_panel < tile_size)
    new_values = jnp.take(new_column, jnp.clip(within_panel, 0, tile_size - 1), axis=1)
    replace_here = column_ok[None, :] & holds_column
    plane_zero = jnp.where(replace_here, new_values, plane_zero)
    return jnp.stack([plane_zero, plane_one, plane_two], axis=1)


def solution(mesh):
    return jax.shard_map(
        body,
        mesh=mesh,
        in_specs=(P("blk", "slab"), P("blk", "slab", None), P("blk", "slab"), P("slab"), P()),
        out_specs=P("blk", None, "slab"),
        check_vma=False,
    )
```

profile of v0, /device:TPU:1, one launch (start us, length us, event | category | flops | bytes accessed | tf_op | source)
XLA Modules:
  0.0 313.2 jit_solution(9936971777019984595)
XLA Ops:
  6.5 3.7 %collective-permute-start.1 = (s32[2,1,8]{2,1,0:T(1,128)}, s32[2,1,8]{2,1,0:T(1,128)S(1)}, u32[]{:S(2)}, u32[]{:S(2)}) collective-permute-start(s32[2,1,8]{2,1,0:T(1,128)} %param.8), channel_id=1, source_target_pairs={{0,4},{4,8},{8,12},{12,16},{16,20},{20,24},{24,28},{28,32},{32,36}... | collective-permute-start | bytes 200 | tf_op jit(solution)/shard_map/ppermute | solution.py:11
  11.3 2.9 collective-permute-start
  21.4 2.3 copy.104
  28.2 2.4 copy.76
  33.0 4.1 %copy.78 = bf16[256,16,256]{0,2,1:T(8,128)(2,1)} copy(bf16[256,16,256]{2,0,1:T(8,128)(2,1)} %select_bitcast_fusion.4) | data formatting | bytes 4194304 | tf_op jit(solution)/shard_map/jit(_take)/select_n | solution.py:49
  37.0 2.4 fusion.19
  42.5 20.7 %collective-permute-done.5 = s32[2,1]{0,1:T(1,128)S(1)} collective-permute-done((s32[2,1]{0,1:T(1,128)S(1)}, s32[2,1]{0,1:T(1,128)S(1)}, u32[]{:S(2)}, u32[]{:S(2)}) %collective-permute-start.5) | collective-permute-done | bytes 40 | tf_op jit(solution)/shard_map/ppermute | solution.py:11
  64.5 7.9 %collective-permute-done.4 = s32[2,1,8]{2,1,0:T(1,128)S(1)} collective-permute-done((s32[2,1,8]{2,1,0:T(1,128)S(1)}, s32[2,1,8]{2,1,0:T(1,128)S(1)}, u32[]{:S(2)}, u32[]{:S(2)}) %collective-permute-start.4) | collective-permute-done | bytes 96 | tf_op jit(solution)/shard_map/ppermute | solution.py:11
  73.7 2.3 copy.105
  80.6 2.4 copy.82
  85.3 4.1 %copy.84 = bf16[256,16,256]{0,2,1:T(8,128)(2,1)} copy(bf16[256,16,256]{2,0,1:T(8,128)(2,1)} %select_bitcast_fusion.2) | data formatting | bytes 4194304 | tf_op jit(solution)/shard_map/jit(_take)/select_n | solution.py:49
  89.4 2.4 fusion.15
  93.8 29.8 %collective-permute-done.3 = bf16[512,2048]{1,0:T(8,128)(2,1)} collective-permute-done((bf16[512,2048]{1,0:T(8,128)(2,1)}, bf16[512,2048]{1,0:T(8,128)(2,1)}, u32[]{:S(2)}, u32[]{:S(2)}) %collective-permute-start.3) | collective-permute-done | bytes 2097184 | tf_op jit(solution)/shard_map/ppermute | solution.py:11
  130.4 2.4 copy.88
  132.8 3.7 %fusion.11 = f32[2,256,256]{2,1,0:T(8,128)} fusion(bf16[256,2,2048]{0,2,1:T(8,128)(2,1)} %bitcast.159, bf16[2,256,2048]{2,1,0:T(8,128)(2,1)} %bitcast.148, f32[2,2048]{1,0:T(2,128)S(1)} %bitcast.177), kind=kOutput, calls=%fused_computation.45 | convolution fusion | flops 540016640 | bytes 4734976 | tf_op jit(solution)/shard_map/axk,zak->axz/dot_general | solution.py:51
  138.8 4.1 %copy.90 = bf16[256,16,256]{0,2,1:T(8,128)(2,1)} copy(bf16[256,16,256]{2,0,1:T(8,128)(2,1)} %select_bitcast_fusion) | data formatting | bytes 4194304 | tf_op jit(solution)/shard_map/jit(_take)/select_n | solution.py:49
  142.9 2.4 fusion.9
  149.9 41.1 %reduce-scatter.2.cloned.1.call-done = f32[512,3,128]{2,0,1:T(8,128)} async-done(((f32[512,3,512]{2,0,1:T(8,128)}), f32[512,3,128]{2,0,1:T(8,128)}) %reduce-scatter.2.cloned.1.call-update) | async-done | bytes 786448 | tf_op jit(solution)/shard_map/reduce_scatter | solution.py:64
  194.1 44.0 %all-reduce.6.cloned.1.call-done = f32[512,256]{0,1:T(8,128)} async-done(((f32[512,256]{0,1:T(8,128)}), f32[512,256]{0,1:T(8,128)}) %all-reduce.6.cloned.1.call-update) | async-done | bytes 524304 | tf_op jit(solution)/shard_map/psum | solution.py:83
  240.2 11.7 %cholesky.50 = f32[128,128]{1,0:T(8,128)S(1)} custom-call(f32[128,128]{1,0:T(8,128)S(1)} %cholesky.118), custom_call_target="Cholesky" | custom-call | tf_op jit(solution)/shard_map/jit(cholesky)/cholesky | solution.py:89
  252.0 9.8 %custom-call.15 = f32[1,128,128]{1,2,0:T(8,128)S(1)} custom-call(f32[1,128,128]{2,1,0:T(8,128)S(1)} %get-tuple-element.43), custom_call_target="InvertDiagBlocksLowerTriangular" | custom-call | tf_op jit(solution)/shard_map/jit(cholesky)/cholesky | solution.py:89
  262.3 11.7 %cholesky.105 = f32[128,128]{1,0:T(8,128)S(1)} custom-call(f32[128,128]{1,0:T(8,128)S(1)} %convolution_subtract_fusion.2), custom_call_target="Cholesky" | custom-call | tf_op jit(solution)/shard_map/jit(cholesky)/cholesky | solution.py:89
  276.9 4.3 %while.1 = (s32[]{:T(128)}, f32[256,256]{1,0:T(8,128)S(1)}, s32[2,2]{1,0:T(2,128)S(1)}, f32[2,128,128]{2,1,0:T(8,128)S(1)}, s32[]{:T(128)}) while((s32[]{:T(128)}, f32[256,256]{1,0:T(8,128)S(1)}, s32[2,2]{1,0:T(2,128)S(1)}, f32[2,128,128]{2,1,0:T(8,128)S(1)}, s32[]{:T(128)}) %tuple.41), condition=%wide.while_cond, body=%wide.while_body.sunk | while | flops 2 | bytes 131181 | solution.py:90
  281.2 19.7 %custom-call.16 = f32[2,128,128]{1,2,0:T(8,128)S(1)} custom-call(f32[2,128,128]{2,1,0:T(8,128)S(1)} %get-tuple-element.13), custom_call_target="InvertDiagBlocksLowerTriangular" | custom-call | tf_op jit(solution)/shard_map/jit(_solve_triangular)/triangular_solve | solution.py:90
  (148 shorter events, 58.9 us)
Async XLA Ops:
  6.5 184.4 %reduce-scatter.2.cloned.1.call-start = ((), (), s32[]{:S(2)}) async-start(), calls=%async_computation.1 | async-start | bytes 3932160 | tf_op jit(solution)/shard_map/reduce_scatter | solution.py:64
  6.5 56.8 %collective-permute-start.1 = (s32[2,1,8]{2,1,0:T(1,128)}, s32[2,1,8]{2,1,0:T(1,128)S(1)}, u32[]{:S(2)}, u32[]{:S(2)}) collective-permute-start(s32[2,1,8]{2,1,0:T(1,128)} %param.8), channel_id=1, source_target_pairs={{0,4},{4,8},{8,12},{12,16},{16,20},{20,24},{24,28},{28,32},{32,36}... | collective-permute-start | bytes 200 | tf_op jit(solution)/shard_map/ppermute | solution.py:11
  10.3 31.1 %collective-permute-start.2 = (s32[2,1]{0,1:T(1,128)}, s32[2,1]{0,1:T(1,128)S(1)}, u32[]{:S(2)}, u32[]{:S(2)}) collective-permute-start(s32[2,1]{0,1:T(1,128)} %param.9), channel_id=1, source_target_pairs={{0,4},{4,8},{8,12},{12,16},{16,20},{20,24},{24,28},{28,32},{32,36}... | collective-permute-start | bytes 32 | tf_op jit(solution)/shard_map/ppermute | solution.py:11
  11.3 62.1 %collective-permute-start = (bf16[512,2048]{1,0:T(8,128)(2,1)}, bf16[512,2048]{1,0:T(8,128)(2,1)}, u32[]{:S(2)}, u32[]{:S(2)}) collective-permute-start(bf16[512,2048]{1,0:T(8,128)(2,1)} %param.7), channel_id=1, source_target_pairs={{0,4},{4,8},{8,12},{12,16},{16,20},{20,24},{24,28},{28,32},{32,36}... | collective-permute-start | bytes 6291464 | tf_op jit(solution)/shard_map/ppermute | solution.py:11
  33.0 4.1 %copy-start.2 = (bf16[512,2048]{1,0:T(8,128)(2,1)S(1)}, bf16[512,2048]{1,0:T(8,128)(2,1)}, u32[]{:S(2)}) copy-start(bf16[512,2048]{1,0:T(8,128)(2,1)} %param.7) | copy-start | bytes 6291460
  37.0 2.5 copy-start.5
  41.5 21.7 %collective-permute-start.5 = (s32[2,1]{0,1:T(1,128)S(1)}, s32[2,1]{0,1:T(1,128)S(1)}, u32[]{:S(2)}, u32[]{:S(2)}) collective-permute-start(s32[2,1]{0,1:T(1,128)S(1)} %collective-permute-done.2), channel_id=1, source_target_pairs={{0,4},{4,8},{8,12},{12,16},{16,20},{20,24},{24,28},{28,32},{32,36}... | collective-permute-start | bytes 32 | tf_op jit(solution)/shard_map/ppermute | solution.py:11
  64.1 8.2 %collective-permute-start.4 = (s32[2,1,8]{2,1,0:T(1,128)S(1)}, s32[2,1,8]{2,1,0:T(1,128)S(1)}, u32[]{:S(2)}, u32[]{:S(2)}) collective-permute-start(s32[2,1,8]{2,1,0:T(1,128)S(1)} %collective-permute-done.1), channel_id=1, source_target_pairs={{0,4},{4,8},{8,12},{12,16},{16,20},{20,24},{24,28},{28,32},{32,36}... | collective-permute-start | bytes 200 | tf_op jit(solution)/shard_map/ppermute | solution.py:11
  73.4 50.1 %collective-permute-start.3 = (bf16[512,2048]{1,0:T(8,128)(2,1)}, bf16[512,2048]{1,0:T(8,128)(2,1)}, u32[]{:S(2)}, u32[]{:S(2)}) collective-permute-start(bf16[512,2048]{1,0:T(8,128)(2,1)} %collective-permute-done), channel_id=1, source_target_pairs={{0,4},{4,8},{8,12},{12,16},{16,20},{20,24},{24,28},{28,32},{32,36}... | collective-permute-start | bytes 6291464 | tf_op jit(solution)/shard_map/ppermute | solution.py:11
  85.3 4.1 %copy-start.3 = (bf16[512,2048]{1,0:T(8,128)(2,1)S(1)}, bf16[512,2048]{1,0:T(8,128)(2,1)}, u32[]{:S(2)}) copy-start(bf16[512,2048]{1,0:T(8,128)(2,1)} %param.7) | copy-start | bytes 6291460
  89.4 2.5 copy-start.6
  138.8 4.1 %copy-start.4 = (bf16[512,2048]{1,0:T(8,128)(2,1)S(1)}, bf16[512,2048]{1,0:T(8,128)(2,1)}, u32[]{:S(2)}) copy-start(bf16[512,2048]{1,0:T(8,128)(2,1)} %param.7) | copy-start | bytes 6291460
  142.9 2.4 copy-start.8
  145.2 1.2 copy-start
  145.3 1.5 copy-start.1
  148.8 89.3 %all-reduce.6.cloned.1.call-start = ((), (), s32[]{:S(2)}) async-start(), calls=%async_computation.2 | async-start | bytes 1048576 | tf_op jit(solution)/shard_map/psum | solution.py:83
  239.0 61.8 %copy-start.7 = (f32[512,256]{0,1:T(8,128)S(1)}, f32[512,256]{0,1:T(8,128)}, u32[]{:S(2)}) copy-start(f32[512,256]{0,1:T(8,128)} %all-reduce.6.cloned.1.call-done) | copy-start | bytes 1572868
  303.5 1.9 slice-start
Sparse Core Ops, SparseCore 0:
  148.9 42.0 reduce-scatter.1
  194.1 43.8 all-reduce.5
where the time goes:
time: 314 us; the launch traced here: 313 us
  waiting for transfers between devices  144 us (46%)
  other arithmetic  79.2 us (25%)
  local copies, waits for them, and re-layouts  49.8 us (16%)
  between operations  16.1 us (5%)
  matrix products  15.2 us (5%)
  starting transfers between devices  9.25 us (3%)
    ppermute x6, waiting for transfers between devices, from_behind(): lax.ppermute(value, axis, [(i, (i + by) % peers) for i in range(peers)])  58.4 us
    psum x1, waiting for transfers between devices, body(): panel_column = lax.psum(panel_piece, 'slab')  44 us
    reduce_scatter x1, waiting for transfers between devices, body(): lax.psum_scatter(partial_band, 'slab', scatter_dimension=2, tiled=True)  41.1 us
    another operation x7, other arithmetic, body(): factor = jnp.linalg.cholesky(pivot_tile)  34.7 us
    another operation x3, other arithmetic, body(): jax.scipy.linalg.solve_triangular(factor, panel_column.T, lower=True)  19.7 us
    select_n x6, local copies, waits for them, and re-layouts, visit_group(): gathered = jnp.take(padded[other_block], slot_index[other_block], axis=1)  19.4 us
    dot_general x6, matrix products, visit_group(): jnp.einsum('axk,zak->axz', flat_scaled, gathered, preferred_element_type=...  12.5 us
    select_n x9, other arithmetic, visit_group(): gathered = jnp.take(padded[other_block], slot_index[other_block], axis=1)  10.5 us
  transfers between devices with their start and end apart: 8, of which 5 were waited for; matrix products, arithmetic and copies ran while one was open for 16% of the time, Pallas kernels for 0%

commit v1 on v0

v1 whole, which is shorter than its diff:
```python
import jax
import jax.numpy as jnp
from jax import lax
from jax.experimental import pallas as pl
from jax.experimental.pallas import tpu as pltpu
from jax.sharding import PartitionSpec as P

ridge_shift = 0.05
AXES = ("blk", "slab")
HIGH = lax.Precision.HIGHEST
SMEM = pl.BlockSpec(memory_space=pltpu.SMEM)
VMEM = pl.BlockSpec(memory_space=pltpu.VMEM)


def product(lhs, rhs, lhs_cols, rhs_cols, scaling, table, scaled, tile, slots, col_tiles, emit):
    for b in range(2):
        for c in range(col_tiles):
            table[b, c] = jnp.int32(slots)
    for b in range(2):
        for n in range(slots):
            col = rhs_cols[b, n]
            table[b, col] = jnp.int32(n)

    def left(t, carry):
        i = t // slots
        m = t % slots
        col = lhs_cols[i, m]
        live = col < col_tiles
        col = jnp.minimum(col, col_tiles - 1)
        other = [table[b, col] for b in range(2)]

        @pl.when(live & ((other[0] < slots) | (other[1] < slots)))
        def _():
            rows = pl.ds(pl.multiple_of(i * tile, tile), tile)
            cols = pl.ds(pl.multiple_of(m * tile, tile), tile)
            scaled[...] = (lhs[rows, cols].astype(jnp.float32) * scaling[pl.ds(col, 1), :]).astype(jnp.bfloat16)
            for b in range(2):

                @pl.when(other[b] < slots)
                def _():
                    cols = pl.ds(pl.multiple_of(other[b] * tile, tile), tile)
                    emit(i, b, lax.dot_general(
                        scaled[...], rhs[b * tile:(b + 1) * tile, cols],
                        (((1,), (1,)), ((), ())), preferred_element_type=jnp.float32))

        return carry

    lax.fori_loop(0, 2 * slots, left, 0)


def own_kernel(tile, slots, col_tiles, cols, scaling, a, far, near, table, scaled):
    y_lo = lax.axis_index("slab") // 2
    far[...] = jnp.zeros_like(far)
    near[...] = jnp.zeros_like(near)

    def emit(i, b, value):
        rows = pl.ds(pl.multiple_of(i * tile, tile), tile)

        @pl.when(b == y_lo)
        def _():
            near[rows, :] += value

        @pl.when(b != y_lo)
        def _():
            far[rows, :] += value

    product(a, a, cols, cols, scaling, table, scaled, tile, slots, col_tiles, emit)


def store_parts(acc, far, near, start):
    y_lo = lax.axis_index("slab") // 2
    size = acc.shape[1]
    far[start:start + size, :] = acc[1 - y_lo].astype(jnp.bfloat16)
    near[start:start + size, :] = acc[y_lo]


def accumulate(acc, tile):
    def emit(i, b, value):
        acc[b, pl.ds(pl.multiple_of(i * tile, tile), tile), :] += value

    return emit


def second_kernel(tile, slots, col_tiles, cols, x_cols, scaling, a, x, far, near, table, scaled, acc):
    core = lax.axis_index("slab") % 2
    acc[...] = jnp.zeros_like(acc)
    emit = accumulate(acc, tile)
    args = (scaling, table, scaled, tile, slots, col_tiles, emit)

    @pl.when(core == 0)
    def _():
        product(a, x, cols, x_cols, *args)

    @pl.when(core == 1)
    def _():
        product(x, a, x_cols, cols, *args)

    store_parts(acc, far, near, 0)


def first_kernel(tile, slots, col_tiles, cols, x_cols, y_cols, scaling, a, x, y, far, near, table, scaled, acc):
    core = lax.axis_index("slab") % 2
    hub = (core + lax.axis_index("blk")) % 2
    emit = accumulate(acc, tile)
    args = (scaling, table, scaled, tile, slots, col_tiles, emit)
    acc[...] = jnp.zeros_like(acc)

    @pl.when((hub == 1) & (core == 0))
    def _():
        product(y, x, y_cols, x_cols, *args)

    @pl.when((hub == 1) & (core == 1))
    def _():
        product(y, a, y_cols, cols, *args)

    store_parts(acc, far, near, 0)
    acc[...] = jnp.zeros_like(acc)

    @pl.when((hub == 1) & (core == 0))
    def _():
        product(a, y, cols, y_cols, *args)

    @pl.when((hub == 1) & (core == 1))
    def _():
        product(x, y, x_cols, y_cols, *args)

    store_parts(acc, far, near, acc.shape[1])


def combine_kernel(near2, got2, near1, got1, cross, ahead, first0, first1, kept):
    core = lax.axis_index("slab") % 2
    rows, width = near2.shape
    half = width // 2
    plane2 = near2[...] + got2[...].astype(jnp.float32)
    plane1 = near1[rows:, :] + got1[rows:, :].astype(jnp.float32)
    other1 = near1[:rows, :] + got1[:rows, :].astype(jnp.float32)
    first0[...] = other1[:, :half].astype(jnp.bfloat16)
    first1[...] = other1[:, half:].astype(jnp.bfloat16)
    for start, value in ((0, plane2), (rows, plane1)):
        mine = jnp.where(core == 0, value[:, :half], value[:, half:])
        theirs = jnp.where(core == 0, value[:, half:], value[:, :half])
        cross[start:start + rows, :] = theirs.astype(jnp.bfloat16)
        ahead[start:start + rows, :] = mine.astype(jnp.bfloat16)
        kept[start:start + rows, :] = mine


def eliminate(matrix, size, group):
    tiles = size // 8
    v = matrix.reshape(tiles, 8, 128)
    ids = lax.broadcasted_iota(jnp.int32, (tiles, 8, 128), 0) * 8 + lax.broadcasted_iota(
        jnp.int32, (tiles, 8, 128), 1)
    pivots = [jnp.ones((8, 128), jnp.float32) for _ in range(tiles)]
    for j in range(0, size, group):
        s = {}
        for a in range(group):
            for b in range(a + 1):
                r = j + a
                s[a, b] = jnp.broadcast_to(v[r // 8, r % 8:r % 8 + 1, j + b:j + b + 1], (8, 128))
        rows = [jnp.broadcast_to(v[(j + a) // 8, (j + a) % 8:(j + a) % 8 + 1, :], (8, 128)) for a in range(group)]
        below = (j + group) // 8
        last = j + group >= size
        cols = [] if last else [
            jnp.broadcast_to(v[below:, :, j + b:j + b + 1], (tiles - below, 8, 128)) for b in range(group)]
        low = {}
        inverse = []
        for b in range(group):
            inverse.append(1.0 / s[b, b])
            for a in range(b + 1, group):
                low[a, b] = s[a, b] * inverse[b]
            for a in range(b + 1, group):
                for c in range(b + 1, a + 1):
                    s[a, c] = s[a, c] - low[a, b] * s[c, b]
        for a in range(group):
            for b in range(a):
                rows[a] = rows[a] - low[a, b] * rows[b]
        top = j // 8
        kept = v[top]
        for a in range(group):
            here = ids[top] == j + a
            kept = jnp.where(here, rows[a], kept)
            pivots[top] = jnp.where(here, s[a, a], pivots[top])
        pieces = [v[:top]] if top else []
        pieces.append(kept[None])
        if not last:
            steps = []
            update = None
            for b in range(group):
                step = cols[b]
                for k in range(b):
                    step = step - steps[k] * s[b, k][None]
                steps.append(step * inverse[b][None])
                term = steps[b] * rows[b][None]
                update = term if update is None else update + term
            pieces.append(v[below:] - update)
        v = jnp.concatenate(pieces, 0) if len(pieces) > 1 else pieces[0]
    return (v * lax.rsqrt(jnp.stack(pivots))).reshape(size, 128)


def panel_factor(w, u, size, group):
    n, width = w.shape
    for start in range(0, n, size):
        base = start // 128 * 128
        square = w[start:start + size, base:base + 128]
        if start > base:
            square = pltpu.roll(square, 128 - (start - base), 1)
        lane = lax.broadcasted_iota(jnp.int32, (size, 128), 1)
        row = lax.broadcasted_iota(jnp.int32, (size, 128), 0)
        square = jnp.where(lane < size, square, jnp.where(lane - size == row, 1.0, 0.0))
        inverse = eliminate(square, size, group)[:, size:2 * size]
        strip = lax.dot_general(
            inverse, w[start:start + size, :], (((1,), (0,)), ((), ())),
            precision=HIGH, preferred_element_type=jnp.float32)
        lane = lax.broadcasted_iota(jnp.int32, (size, width), 1)
        row = lax.broadcasted_iota(jnp.int32, (size, width), 0)
        strip = jnp.where(lane - start >= row, strip, 0.0)
        u[start:start + size, :] = strip
        if start + size < n:
            w[start + size:, :] = w[start + size:, :] - lax.dot_general(
                strip[:, start + size:n], strip, (((0,), (0,)), ((), ())),
                precision=HIGH, preferred_element_type=jnp.float32)


def panel_kernel(tile, panel, part, other, column, lower, total, w, u):
    slab = lax.axis_index("slab")
    core = slab % 2
    y_lo = slab // 2
    half = tile // 2
    block = panel[0]
    pos = block % 2
    holds = (block // 2 == lax.axis_index("blk")) & (pos == y_lo)
    total[...] = part[...] + other[...]
    eye = jnp.where(
        lax.broadcasted_iota(jnp.int32, (tile, tile), 0) == lax.broadcasted_iota(jnp.int32, (tile, tile), 1),
        jnp.float32(ridge_shift), jnp.float32(0.0))
    total[pl.ds(pl.multiple_of(y_lo * tile, tile), tile), :] += eye

    @pl.when(jnp.logical_not(holds))
    def _():
        lower[...] = jnp.zeros_like(lower)

        @pl.when(core == 0)
        def _():
            column[...] = total[:, :half]

        @pl.when(core == 1)
        def _():
            column[...] = total[:, half:]

    @pl.when(holds)
    def _():
        pivot_rows = pl.ds(pl.multiple_of(pos * tile, tile), tile)
        other_rows = pl.ds(pl.multiple_of((1 - pos) * tile, tile), tile)
        square = total[pivot_rows, :]
        w[:, :tile] = (square + square.T) * 0.5
        w[:, tile:] = total[other_rows, :].T
        panel_factor(w, u, 64, 8)
        lower[...] = u[:, tile:].astype(lower.dtype)
        rows = pl.ds(pl.multiple_of(core * half, half), half)
        column[pivot_rows, :] = u[rows, :tile].T
        column[other_rows, :] = u[rows, tile:].T


def final_kernel(tile, panel, column, lower, kept, cross, ahead, first0, first1, out):
    slab = lax.axis_index("slab")
    core = slab % 2
    y_lo = slab // 2
    half = tile // 2
    group = lax.axis_index("blk")
    odd = group % 2
    rows = column.shape[0]
    block = panel[0]
    pos = block % 2
    out[0] = column[...]

    @pl.when((block // 2 == group) & (pos != y_lo))
    def _():
        left = lower[...].astype(jnp.float32)
        right = jnp.where(core == 0, left[:, :half], left[:, half:])
        here = pl.ds(pl.multiple_of(y_lo * tile, tile), tile)
        out[0, here, :] = out[0, here, :] - lax.dot_general(
            left, right, (((0,), (0,)), ((), ())), precision=HIGH, preferred_element_type=jnp.float32)

    wide = lambda ref, start: ref[start:start + rows, :].astype(jnp.float32)

    @pl.when(core == 0)
    def _():
        out[2] = kept[:rows, :] + wide(cross, 0)

        @pl.when(odd == 1)
        def _():
            out[1] = kept[rows:, :] + wide(first0, 0)

        @pl.when(odd == 0)
        def _():
            out[1] = wide(cross, rows) + wide(first0, 0)

    @pl.when(core == 1)
    def _():
        out[2] = wide(ahead, 0) + wide(cross, 0)

        @pl.when(odd == 1)
        def _():
            out[1] = wide(cross, rows) + wide(first1, 0)

        @pl.when(odd == 0)
        def _():
            out[1] = wide(ahead, rows) + wide(first1, 0)


def make_body(groups, slabs):
    devices = [(g, s) for g in range(groups) for s in range(slabs)]
    at = lambda g, s: (g % groups) * slabs + s
    forward = lambda s: s % 2 == 0
    hubs = [(g, s) for g, s in devices if (g + s) % 2 == 1]
    far_pairs = [(at(g, s), at(g + (2 if forward(s) else -2), s)) for g, s in devices]
    near_pairs = [(at(g + (-1 if forward(s) else 1), s), at(g, s)) for g, s in hubs]
    chip_pairs = [(at(g, s), at(g, s ^ 2)) for g, s in devices]
    chip_hub_pairs = [(at(g, s), at(g, s ^ 2)) for g, s in hubs]
    core_pairs = [(at(g, s), at(g, s ^ 1)) for g, s in devices]
    cross_pairs = [(at(g, s), at(g, s + 1) if forward(s) else at(g + 2, s - 1)) for g, s in devices]
    ahead_pairs = [(at(g, s), at(g + 2, s)) for g, s in devices if not forward(s)]
    first0_pairs = [(at(g, s), at(g - 1, s) if forward(s) else at(g + 1, s - 1)) for g, s in hubs]
    first1_pairs = [(at(g, s), at(g - 1, s + 1) if forward(s) else at(g + 1, s)) for g, s in hubs]

    def move(value, pairs):
        return lax.ppermute(value, AXES, pairs)

    def body(a_tiles, tile_cols, tile_counts, scaling, panel):
        rows = a_tiles.shape[0]
        blocks = tile_cols.shape[0]
        slots = tile_cols.shape[2]
        tile = rows // blocks
        col_tiles = scaling.shape[0] // tile
        half = tile // 2
        f32 = jnp.float32
        bf16 = jnp.bfloat16
        shape = jax.ShapeDtypeStruct
        slot_ids = jnp.arange(slots, dtype=jnp.int32)
        cols = jnp.where(slot_ids[None, :] < tile_counts, tile_cols[:, 0, :], col_tiles)
        scales = scaling.reshape(col_tiles, tile)
        x = move(a_tiles, far_pairs)
        y = move(a_tiles, near_pairs)
        x_cols = move(cols, far_pairs)
        y_cols = move(cols, near_pairs)
        table = pltpu.SMEM((2, col_tiles + 1), jnp.int32)
        scaled = pltpu.VMEM((tile, tile), bf16)
        acc = pltpu.VMEM((2, rows, tile), f32)
        sizes = (tile, slots, col_tiles)
        far0, near0 = pl.pallas_call(
            lambda *refs: own_kernel(*sizes, *refs),
            out_shape=(shape((rows, tile), f32), shape((rows, tile), f32)),
            in_specs=[SMEM, VMEM, VMEM], out_specs=(VMEM, VMEM),
            scratch_shapes=[table, scaled], name="plane_zero",
        )(cols, scales, a_tiles)
        part = near0 + move(far0, chip_pairs)
        other = move(part, core_pairs)
        column, lower = pl.pallas_call(
            lambda *refs: panel_kernel(tile, *refs),
            out_shape=(shape((rows, half), f32), shape((tile, tile), bf16)),
            in_specs=[SMEM, VMEM, VMEM], out_specs=(VMEM, VMEM),
            scratch_shapes=[pltpu.VMEM((rows, tile), f32), pltpu.VMEM((tile, rows), f32), pltpu.VMEM((tile, rows), f32)],
            name="panel_step",
        )(panel, part, other)
        lower = move(lower, chip_pairs)
        far2, near2 = pl.pallas_call(
            lambda *refs: second_kernel(*sizes, *refs),
            out_shape=(shape((rows, tile), bf16), shape((rows, tile), f32)),
            in_specs=[SMEM, SMEM, VMEM, VMEM, VMEM], out_specs=(VMEM, VMEM),
            scratch_shapes=[table, scaled, acc], name="plane_two",
        )(cols, x_cols, scales, a_tiles, x)
        got2 = move(far2, chip_pairs)
        far1, near1 = pl.pallas_call(
            lambda *refs: first_kernel(*sizes, *refs),
            out_shape=(shape((2 * rows, tile), bf16), shape((2 * rows, tile), f32)),
            in_specs=[SMEM, SMEM, SMEM, VMEM, VMEM, VMEM, VMEM], out_specs=(VMEM, VMEM),
            scratch_shapes=[table, scaled, acc], name="plane_one",
        )(cols, x_cols, y_cols, scales, a_tiles, x, y)
        got1 = move(far1, chip_hub_pairs)
        cross, ahead, first0, first1, kept = pl.pallas_call(
            combine_kernel,
            out_shape=(shape((2 * rows, half), bf16), shape((2 * rows, half), bf16), shape((rows, half), bf16),
                       shape((rows, half), bf16), shape((2 * rows, half), f32)),
            in_specs=[VMEM] * 4, out_specs=(VMEM,) * 5, name="combine",
        )(near2, got2, near1, got1)
        cross = move(cross, cross_pairs)
        ahead = move(ahead, ahead_pairs)
        first0 = move(first0, first0_pairs)
        first1 = move(first1, first1_pairs)
        out = pl.pallas_call(
            lambda *refs: final_kernel(tile, *refs),
            out_shape=shape((3, rows, half), f32),
            in_specs=[SMEM] + [VMEM] * 7, out_specs=VMEM, name="assemble",
        )(panel, column, lower, kept, cross, ahead, first0, first1)
        return out.transpose(1, 0, 2)

    return body


def solution(mesh):
    return jax.shard_map(
        make_body(mesh.shape["blk"], mesh.shape["slab"]),
        mesh=mesh,
        in_specs=(P("blk", "slab"), P("blk", "slab", None), P("blk", "slab"), P("slab"), P()),
        out_specs=P("blk", None, "slab"),
        check_vma=False,
    )
```

time: 314 us -> 105 us (0.33)
  the two profiles are of different devices: /device:TPU:1 before, /device:TPU:161 now
where the time goes in v1:
time: 105 us
  waiting for transfers between devices  42.4 us (40%)
  starting transfers between devices  31.2 us (30%)
  Pallas kernels  23.7 us (23%)
  local copies, waits for them, and re-layouts  5.19 us (5%)
  other arithmetic  1.39 us (1%)
    ppermute x13, waiting for transfers between devices, move(): return lax.ppermute(value, AXES, pairs)  42.4 us
    ppermute x13, starting transfers between devices, move(): return lax.ppermute(value, AXES, pairs)  31.2 us
    pallas_call x1, Pallas kernels, body(): pl.pallas_call(lambda *refs: first_kernel(*sizes, *refs), out_shape=(shap...  6.85 us
    pallas_call x1, Pallas kernels, body(): pl.pallas_call(lambda *refs: second_kernel(*sizes, *refs), out_shape=(sha...  4.89 us
    pallas_call x1, Pallas kernels, body(): pl.pallas_call(lambda *refs: own_kernel(*sizes, *refs), out_shape=(shape(...  4.51 us
    unnamed x28, local copies, waits for them, and re-layouts  3.87 us
    pallas_call x1, Pallas kernels, body(): pl.pallas_call(combine_kernel, out_shape=(shape((2 * rows, half), bf16),...  2.78 us
    pallas_call x1, Pallas kernels, body(): pl.pallas_call(lambda *refs: final_kernel(tile, *refs), out_shape=shape((...  2.39 us
  transfers between devices with their start and end apart: 13, of which 5 were waited for; matrix products, arithmetic and copies ran while one was open for 3% of the time, Pallas kernels for 20%

profile of v1, /device:TPU:161, one launch (start us, length us, event | category | flops | bytes accessed | tf_op | source)
XLA Modules:
  0.0 104.7 jit_solution(8768070771475050358)
XLA Ops:
  0.0 2.9 %collective-permute-start.4 = (bf16[512,2048]{1,0:T(8,128)(2,1)}, bf16[512,2048]{1,0:T(8,128)(2,1)S(1)}, u32[]{:S(2)}, u32[]{:S(2)}) collective-permute-start(bf16[512,2048]{1,0:T(8,128)(2,1)} %refs_4_.1), channel_id=1, source_target_pairs={{0,8},{1,249},{2,10},{3,251},{4,12},{5,253},{6,14},{7,255},{8,16},... | collective-permute-start | bytes 6291464 | tf_op jit(solution)/shard_map/ppermute | solution.py:326
  2.9 1.3 %collective-permute-start.7 = (bf16[512,2048]{1,0:T(8,128)(2,1)}, bf16[512,2048]{1,0:T(8,128)(2,1)}, u32[]{:S(2)}, u32[]{:S(2)}) collective-permute-start(bf16[512,2048]{1,0:T(8,128)(2,1)} %refs_4_.1), channel_id=1, source_target_pairs={{5,1},{7,3},{0,4},{2,6},{13,9},{15,11},{8,12},{10,14},{21,17},{23,... | collective-permute-start | bytes 6291464 | tf_op jit(solution)/shard_map/ppermute | solution.py:326
  4.2 1.3 %reshape.3.refs_1_.refs_2_.refs_3_ = f32[16,256]{1,0:T(8,128)} reshape(f32[4096]{0:T(1024)} %param.8) | data formatting | bytes 32768 | tf_op jit(solution)/shard_map/reshape | solution.py:340
  5.5 1.3 %compare_select_fusion.refs_0_ = s32[2,8]{1,0:T(2,128)} fusion(s32[2,8]{1,0:T(2,128)} %bitcast.3, s32[2]{0:T(128)} %bitcast.4), kind=kLoop, calls=%fused_computation | loop fusion | flops 32 | bytes 136 | tf_op jit(solution)/shard_map/jit(_where)/select_n | solution.py:339
  6.9 4.5 %plane_zero.1 = (f32[512,256]{1,0:T(8,128)}, f32[512,256]{1,0:T(8,128)}) custom-call(s32[2,8]{1,0:T(2,128)} %compare_select_fusion.refs_0_, f32[16,256]{1,0:T(8,128)} %reshape.3.refs_1_.refs_2_.refs_3_, bf16[512,2048]{1,0:T(8,128)(2,1)} %refs_4_.1), custom_call_target="tpu_custom_call" | custom-call | tf_op jit(solution)/shard_map/plane_zero/pallas_call | solution.py:349
  11.4 2.0 %collective-permute-start = (f32[512,256]{1,0:T(8,128)}, f32[512,256]{1,0:T(8,128)S(1)}, u32[]{:S(2)}, u32[]{:S(2)}) collective-permute-start(f32[512,256]{1,0:T(8,128)} %get-tuple-element.19), channel_id=1, source_target_pairs={{0,2},{1,3},{2,0},{3,1},{4,6},{5,7},{6,4},{7,5},{8,10},{9,11},{10,... | collective-permute-start | bytes 1572872 | tf_op jit(solution)/shard_map/ppermute | solution.py:326
  13.4 1.3 %collective-permute-start.6 = (s32[2,8]{1,0:T(2,128)S(1)}, s32[2,8]{1,0:T(2,128)S(1)}, u32[]{:S(2)}, u32[]{:S(2)}) collective-permute-start(s32[2,8]{1,0:T(2,128)S(1)} %copy-done.11), channel_id=1, source_target_pairs={{5,1},{7,3},{0,4},{2,6},{13,9},{15,11},{8,12},{10,14},{21,17},{23,... | collective-permute-start | bytes 200 | tf_op jit(solution)/shard_map/ppermute | solution.py:326
  14.7 11.5 %collective-permute-done.3.refs_1_ = s32[2,8]{1,0:T(2,128)S(1)} collective-permute-done((s32[2,8]{1,0:T(2,128)S(1)}, s32[2,8]{1,0:T(2,128)S(1)}, u32[]{:S(2)}, u32[]{:S(2)}) %collective-permute-start.3) | collective-permute-done | bytes 96 | tf_op jit(solution)/shard_map/ppermute | solution.py:326
  26.2 16.4 %collective-permute-done.6.refs_2_ = s32[2,8]{1,0:T(2,128)S(1)} collective-permute-done((s32[2,8]{1,0:T(2,128)S(1)}, s32[2,8]{1,0:T(2,128)S(1)}, u32[]{:S(2)}, u32[]{:S(2)}) %collective-permute-start.6) | collective-permute-done | bytes 96 | tf_op jit(solution)/shard_map/ppermute | solution.py:326
  43.2 0.8 copy-done
  44.0 6.9 %plane_one.1 = (bf16[1024,256]{1,0:T(8,128)(2,1)}, f32[1024,256]{1,0:T(8,128)}) custom-call(s32[2,8]{1,0:T(2,128)} %compare_select_fusion.refs_0_, s32[2,8]{1,0:T(2,128)} %copy-done.12, s32[2,8]{1,0:T(2,128)} %copy-done.13, f32[16,256]{1,0:T(8,128)} %reshape.3.refs_1_.refs_2_.refs_3_, bf16[512,2048]{1,0:T(8,128)(2,1)} %refs_4_.1, bf16[512,2048]{1,0:T(8,128)(2,1)} %copy-done, ...), custom_call_target="tpu_custom_call" | custom-call | tf_op jit(solution)/shard_map/plane_one/pallas_call | solution.py:372
  50.9 2.7 %collective-permute-start.8 = (bf16[1024,256]{1,0:T(8,128)(2,1)}, bf16[1024,256]{1,0:T(8,128)(2,1)S(1)}, u32[]{:S(2)}, u32[]{:S(2)}) collective-permute-start(bf16[1024,256]{1,0:T(8,128)(2,1)} %get-tuple-element.25), channel_id=1, source_target_pairs={{1,3},{3,1},{4,6},{6,4},{9,11},{11,9},{12,14},{14,12},{17,19},{19,... | collective-permute-start | bytes 1572872 | tf_op jit(solution)/shard_map/ppermute | solution.py:326
  53.8 4.9 %plane_two.1 = (bf16[512,256]{1,0:T(8,128)(2,1)}, f32[512,256]{1,0:T(8,128)}) custom-call(s32[2,8]{1,0:T(2,128)} %compare_select_fusion.refs_0_, s32[2,8]{1,0:T(2,128)} %copy-done.12, f32[16,256]{1,0:T(8,128)} %reshape.3.refs_1_.refs_2_.refs_3_, bf16[512,2048]{1,0:T(8,128)(2,1)} %refs_4_.1, bf16[512,2048]{1,0:T(8,128)(2,1)} %copy-done), custom_call_target="tpu_custom_call" | custom-call | tf_op jit(solution)/shard_map/plane_two/pallas_call | solution.py:365
  58.7 8.4 %collective-permute-done.5.got2 = bf16[512,256]{1,0:T(8,128)(2,1)S(1)} collective-permute-done((bf16[512,256]{1,0:T(8,128)(2,1)}, bf16[512,256]{1,0:T(8,128)(2,1)S(1)}, u32[]{:S(2)}, u32[]{:S(2)}) %collective-permute-start.5) | collective-permute-done | bytes 262176 | tf_op jit(solution)/shard_map/ppermute | solution.py:326
  67.1 0.7 copy-done.5
  68.0 2.8 %combine.1 = (bf16[1024,128]{1,0:T(8,128)(2,1)}, bf16[1024,128]{1,0:T(8,128)(2,1)}, bf16[512,128]{1,0:T(8,128)(2,1)}, bf16[512,128]{1,0:T(8,128)(2,1)}, f32[1024,128]{1,0:T(8,128)}) custom-call(f32[512,256]{1,0:T(8,128)} %get-tuple-element.22.near2, bf16[512,256]{1,0:T(8,128)(2,1)} %copy-done.5, f32[1024,256]{1,0:T(8,128)} %get-tuple-element.24.near1, ...), custom_call_target="tpu_custom_call" | custom-call | tf_op jit(solution)/shard_map/combine/pallas_call | solution.py:379
  70.8 1.9 %collective-permute-start.10 = (bf16[1024,128]{1,0:T(8,128)(2,1)}, bf16[1024,128]{1,0:T(8,128)(2,1)S(1)}, u32[]{:S(2)}, u32[]{:S(2)}) collective-permute-start(bf16[1024,128]{1,0:T(8,128)(2,1)} %get-tuple-element.28), channel_id=1, source_target_pairs={{1,9},{3,11},{5,13},{7,15},{9,17},{11,19},{13,21},{15,23},{17,25},... | collective-permute-start | bytes 786440 | tf_op jit(solution)/shard_map/ppermute | solution.py:326
  73.5 0.8 copy-done.3
  74.3 2.2 %panel_step.1 = (f32[512,128]{1,0:T(8,128)}, bf16[256,256]{1,0:T(8,128)(2,1)}) custom-call(s32[1]{0:T(128)S(6)} %copy.6.refs_0_, f32[512,256]{1,0:T(8,128)} %copy-done.1, f32[512,256]{1,0:T(8,128)} %copy-done.3), custom_call_target="tpu_custom_call" | custom-call | tf_op jit(solution)/shard_map/panel_step/pallas_call | solution.py:357
  76.5 16.9 %collective-permute-start.11 = (bf16[512,128]{1,0:T(8,128)(2,1)}, bf16[512,128]{1,0:T(8,128)(2,1)S(1)}, u32[]{:S(2)}, u32[]{:S(2)}) collective-permute-start(bf16[512,128]{1,0:T(8,128)(2,1)} %get-tuple-element.29), channel_id=1, source_target_pairs={{1,4},{3,6},{4,0},{6,2},{9,12},{11,14},{12,8},{14,10},{17,20},{19,... | collective-permute-start | bytes 393224 | tf_op jit(solution)/shard_map/ppermute | solution.py:326
  93.5 1.9 %collective-permute-start.12 = (bf16[512,128]{1,0:T(8,128)(2,1)}, bf16[512,128]{1,0:T(8,128)(2,1)S(1)}, u32[]{:S(2)}, u32[]{:S(2)}) collective-permute-start(bf16[512,128]{1,0:T(8,128)(2,1)} %get-tuple-element.30), channel_id=1, source_target_pairs={{1,5},{3,7},{4,1},{6,3},{9,13},{11,15},{12,9},{14,11},{17,21},{19,... | collective-permute-start | bytes 393224 | tf_op jit(solution)/shard_map/ppermute | solution.py:326
  95.7 5.8 %collective-permute-done.12.refs_7_ = bf16[512,128]{1,0:T(8,128)(2,1)S(1)} collective-permute-done((bf16[512,128]{1,0:T(8,128)(2,1)}, bf16[512,128]{1,0:T(8,128)(2,1)S(1)}, u32[]{:S(2)}, u32[]{:S(2)}) %collective-permute-start.12) | collective-permute-done | bytes 131104 | tf_op jit(solution)/shard_map/ppermute | solution.py:326
  101.5 0.6 copy-done.10
  102.3 2.4 %assemble.1 = f32[3,512,128]{2,1,0:T(8,128)} custom-call(s32[1]{0:T(128)S(6)} %copy.6.refs_0_, f32[512,128]{1,0:T(8,128)} %get-tuple-element.20.refs_1_, bf16[256,256]{1,0:T(8,128)(2,1)} %copy-done.8, f32[1024,128]{1,0:T(8,128)} %get-tuple-element.26.refs_3_, bf16[1024,128]{1,0:T(8,128)(2,1)} %copy-done.7, bf16[1024,128]{1,0:T(8,128)(2,1)} %copy-done.6, ...), custom_call_target="tpu_custom_call" | custom-call | tf_op jit(solution)/shard_map/assemble/pallas_call | solution.py:389
  (39 shorter events, 1.5 us)
Async XLA Ops:
  0.0 42.7 %collective-permute-start.4 = (bf16[512,2048]{1,0:T(8,128)(2,1)}, bf16[512,2048]{1,0:T(8,128)(2,1)S(1)}, u32[]{:S(2)}, u32[]{:S(2)}) collective-permute-start(bf16[512,2048]{1,0:T(8,128)(2,1)} %refs_4_.1), channel_id=1, source_target_pairs={{0,8},{1,249},{2,10},{3,251},{4,12},{5,253},{6,14},{7,255},{8,16},... | collective-permute-start | bytes 6291464 | tf_op jit(solution)/shard_map/ppermute | solution.py:326
  2.9 39.7 %collective-permute-start.7 = (bf16[512,2048]{1,0:T(8,128)(2,1)}, bf16[512,2048]{1,0:T(8,128)(2,1)}, u32[]{:S(2)}, u32[]{:S(2)}) collective-permute-start(bf16[512,2048]{1,0:T(8,128)(2,1)} %refs_4_.1), channel_id=1, source_target_pairs={{5,1},{7,3},{0,4},{2,6},{13,9},{15,11},{8,12},{10,14},{21,17},{23,... | collective-permute-start | bytes 6291464 | tf_op jit(solution)/shard_map/ppermute | solution.py:326
  6.9 6.6 %copy-start.11 = (s32[2,8]{1,0:T(2,128)S(1)}, s32[2,8]{1,0:T(2,128)}, u32[]{:S(2)}) copy-start(s32[2,8]{1,0:T(2,128)} %compare_select_fusion.refs_0_) | copy-start | bytes 196
  11.4 42.2 %copy-start.2 = (f32[512,256]{1,0:T(8,128)S(1)}, f32[512,256]{1,0:T(8,128)}, u32[]{:S(2)}) copy-start(f32[512,256]{1,0:T(8,128)} %get-tuple-element.18) | copy-start | bytes 1572868
  11.4 42.2 %collective-permute-start = (f32[512,256]{1,0:T(8,128)}, f32[512,256]{1,0:T(8,128)S(1)}, u32[]{:S(2)}, u32[]{:S(2)}) collective-permute-start(f32[512,256]{1,0:T(8,128)} %get-tuple-element.19), channel_id=1, source_target_pairs={{0,2},{1,3},{2,0},{3,1},{4,6},{5,7},{6,4},{7,5},{8,10},{9,11},{10,... | collective-permute-start | bytes 1572872 | tf_op jit(solution)/shard_map/ppermute | solution.py:326
  13.4 12.8 %collective-permute-start.3 = (s32[2,8]{1,0:T(2,128)S(1)}, s32[2,8]{1,0:T(2,128)S(1)}, u32[]{:S(2)}, u32[]{:S(2)}) collective-permute-start(s32[2,8]{1,0:T(2,128)S(1)} %copy-done.11), channel_id=1, source_target_pairs={{0,8},{1,249},{2,10},{3,251},{4,12},{5,253},{6,14},{7,255},{8,16},... | collective-permute-start | bytes 200 | tf_op jit(solution)/shard_map/ppermute | solution.py:326
  13.4 29.2 %collective-permute-start.6 = (s32[2,8]{1,0:T(2,128)S(1)}, s32[2,8]{1,0:T(2,128)S(1)}, u32[]{:S(2)}, u32[]{:S(2)}) collective-permute-start(s32[2,8]{1,0:T(2,128)S(1)} %copy-done.11), channel_id=1, source_target_pairs={{5,1},{7,3},{0,4},{2,6},{13,9},{15,11},{8,12},{10,14},{21,17},{23,... | collective-permute-start | bytes 200 | tf_op jit(solution)/shard_map/ppermute | solution.py:326
  26.2 16.4 %copy-start.12 = (s32[2,8]{1,0:T(2,128)}, s32[2,8]{1,0:T(2,128)S(1)}, u32[]{:S(2)}) copy-start(s32[2,8]{1,0:T(2,128)S(1)} %collective-permute-done.3.refs_1_) | copy-start | bytes 196
  42.7 1.3 %copy-start = (bf16[512,2048]{1,0:T(8,128)(2,1)}, bf16[512,2048]{1,0:T(8,128)(2,1)S(1)}, u32[]{:S(2)}) copy-start(bf16[512,2048]{1,0:T(8,128)(2,1)S(1)} %collective-permute-done.4.refs_4_.refs_5_) | copy-start | bytes 6291460
  50.9 16.3 %collective-permute-start.8 = (bf16[1024,256]{1,0:T(8,128)(2,1)}, bf16[1024,256]{1,0:T(8,128)(2,1)S(1)}, u32[]{:S(2)}, u32[]{:S(2)}) collective-permute-start(bf16[1024,256]{1,0:T(8,128)(2,1)} %get-tuple-element.25), channel_id=1, source_target_pairs={{1,3},{3,1},{4,6},{6,4},{9,11},{11,9},{12,14},{14,12},{17,19},{19,... | collective-permute-start | bytes 1572872 | tf_op jit(solution)/shard_map/ppermute | solution.py:326
  53.7 5.0 %copy-start.1 = (f32[512,256]{1,0:T(8,128)}, f32[512,256]{1,0:T(8,128)S(1)}, u32[]{:S(2)}) copy-start(f32[512,256]{1,0:T(8,128)S(1)} %add.3.refs_1_) | copy-start | bytes 1572868
  53.7 19.8 %collective-permute-start.1 = (f32[512,256]{1,0:T(8,128)S(1)}, f32[512,256]{1,0:T(8,128)S(1)}, u32[]{:S(2)}, u32[]{:S(2)}) collective-permute-start(f32[512,256]{1,0:T(8,128)S(1)} %add.3.refs_1_), channel_id=1, source_target_pairs={{0,1},{1,0},{2,3},{3,2},{4,5},{5,4},{6,7},{7,6},{8,9},{9,8},{10,11... | collective-permute-start | bytes 1572872 | tf_op jit(solution)/shard_map/ppermute | solution.py:326
  58.7 8.4 %collective-permute-start.5 = (bf16[512,256]{1,0:T(8,128)(2,1)}, bf16[512,256]{1,0:T(8,128)(2,1)S(1)}, u32[]{:S(2)}, u32[]{:S(2)}) collective-permute-start(bf16[512,256]{1,0:T(8,128)(2,1)} %get-tuple-element.23), channel_id=1, source_target_pairs={{0,2},{1,3},{2,0},{3,1},{4,6},{5,7},{6,4},{7,5},{8,10},{9,11},{10,... | collective-permute-start | bytes 786440 | tf_op jit(solution)/shard_map/ppermute | solution.py:326
  67.1 0.9 copy-start.4
  70.8 30.7 %collective-permute-start.10 = (bf16[1024,128]{1,0:T(8,128)(2,1)}, bf16[1024,128]{1,0:T(8,128)(2,1)S(1)}, u32[]{:S(2)}, u32[]{:S(2)}) collective-permute-start(bf16[1024,128]{1,0:T(8,128)(2,1)} %get-tuple-element.28), channel_id=1, source_target_pairs={{1,9},{3,11},{5,13},{7,15},{9,17},{11,19},{13,21},{15,23},{17,25},... | collective-permute-start | bytes 786440 | tf_op jit(solution)/shard_map/ppermute | solution.py:326
  72.7 28.8 %collective-permute-start.9 = (bf16[1024,128]{1,0:T(8,128)(2,1)}, bf16[1024,128]{1,0:T(8,128)(2,1)S(1)}, u32[]{:S(2)}, u32[]{:S(2)}) collective-permute-start(bf16[1024,128]{1,0:T(8,128)(2,1)} %get-tuple-element.27), channel_id=1, source_target_pairs={{0,1},{1,8},{2,3},{3,10},{4,5},{5,12},{6,7},{7,14},{8,9},{9,16},{1... | collective-permute-start | bytes 786440 | tf_op jit(solution)/shard_map/ppermute | solution.py:326
  73.5 0.8 copy-start.3
  76.5 18.9 %collective-permute-start.2 = (bf16[256,256]{1,0:T(8,128)(2,1)}, bf16[256,256]{1,0:T(8,128)(2,1)S(1)}, u32[]{:S(2)}, u32[]{:S(2)}) collective-permute-start(bf16[256,256]{1,0:T(8,128)(2,1)} %get-tuple-element.21), channel_id=1, source_target_pairs={{0,2},{1,3},{2,0},{3,1},{4,6},{5,7},{6,4},{7,5},{8,10},{9,11},{10,... | collective-permute-start | bytes 393224 | tf_op jit(solution)/shard_map/ppermute | solution.py:326
  76.5 19.2 %collective-permute-start.11 = (bf16[512,128]{1,0:T(8,128)(2,1)}, bf16[512,128]{1,0:T(8,128)(2,1)S(1)}, u32[]{:S(2)}, u32[]{:S(2)}) collective-permute-start(bf16[512,128]{1,0:T(8,128)(2,1)} %get-tuple-element.29), channel_id=1, source_target_pairs={{1,4},{3,6},{4,0},{6,2},{9,12},{11,14},{12,8},{14,10},{17,20},{19,... | collective-permute-start | bytes 393224 | tf_op jit(solution)/shard_map/ppermute | solution.py:326
  93.5 8.0 %collective-permute-start.12 = (bf16[512,128]{1,0:T(8,128)(2,1)}, bf16[512,128]{1,0:T(8,128)(2,1)S(1)}, u32[]{:S(2)}, u32[]{:S(2)}) collective-permute-start(bf16[512,128]{1,0:T(8,128)(2,1)} %get-tuple-element.30), channel_id=1, source_target_pairs={{1,5},{3,7},{4,1},{6,3},{9,13},{11,15},{12,9},{14,11},{17,21},{19,... | collective-permute-start | bytes 393224 | tf_op jit(solution)/shard_map/ppermute | solution.py:326
  95.4 6.1 %copy-start.8 = (bf16[256,256]{1,0:T(8,128)(2,1)}, bf16[256,256]{1,0:T(8,128)(2,1)S(1)}, u32[]{:S(2)}) copy-start(bf16[256,256]{1,0:T(8,128)(2,1)S(1)} %collective-permute-done.2.refs_2_) | copy-start | bytes 393220
  95.7 5.8 %copy-start.9 = (bf16[512,128]{1,0:T(8,128)(2,1)}, bf16[512,128]{1,0:T(8,128)(2,1)S(1)}, u32[]{:S(2)}) copy-start(bf16[512,128]{1,0:T(8,128)(2,1)S(1)} %collective-permute-done.11.refs_6_) | copy-start | bytes 393220
  101.5 0.7 copy-start.6
  101.5 0.8 copy-start.7
  (3 other events, 1.9 us)

commit v2 on v1

--- a/solution.py
+++ b/solution.py
@@ -9,6 +9,7 @@
 AXES = ("blk", "slab")
 HIGH = lax.Precision.HIGHEST
 SMEM = pl.BlockSpec(memory_space=pltpu.SMEM)
+ANY = pl.BlockSpec(memory_space=pl.ANY)
 VMEM = pl.BlockSpec(memory_space=pltpu.VMEM)
 
 
@@ -48,100 +49,120 @@
     lax.fori_loop(0, 2 * slots, left, 0)
 
 
-def own_kernel(tile, slots, col_tiles, cols, scaling, a, far, near, table, scaled):
-    y_lo = lax.axis_index("slab") // 2
-    far[...] = jnp.zeros_like(far)
-    near[...] = jnp.zeros_like(near)
-
-    def emit(i, b, value):
-        rows = pl.ds(pl.multiple_of(i * tile, tile), tile)
-
-        @pl.when(b == y_lo)
-        def _():
-            near[rows, :] += value
-
-        @pl.when(b != y_lo)
-        def _():
-            far[rows, :] += value
-
-    product(a, a, cols, cols, scaling, table, scaled, tile, slots, col_tiles, emit)
-
-
-def store_parts(acc, far, near, start):
-    y_lo = lax.axis_index("slab") // 2
-    size = acc.shape[1]
-    far[start:start + size, :] = acc[1 - y_lo].astype(jnp.bfloat16)
-    near[start:start + size, :] = acc[y_lo]
-
-
-def accumulate(acc, tile):
+def own_kernel(tile, slots, col_tiles, cols, scaling, a, give, keep, table, scaled, acc):
+    slab = lax.axis_index("slab")
+    core = slab % 2
+    y_lo = slab // 2
+    rows = acc.shape[1]
+    acc[...] = jnp.zeros_like(acc)
+
     def emit(i, b, value):
         acc[b, pl.ds(pl.multiple_of(i * tile, tile), tile), :] += value
 
-    return emit
-
-
-def second_kernel(tile, slots, col_tiles, cols, x_cols, scaling, a, x, far, near, table, scaled, acc):
-    core = lax.axis_index("slab") % 2
-    acc[...] = jnp.zeros_like(acc)
-    emit = accumulate(acc, tile)
-    args = (scaling, table, scaled, tile, slots, col_tiles, emit)
-
-    @pl.when(core == 0)
-    def _():
-        product(a, x, cols, x_cols, *args)
-
-    @pl.when(core == 1)
-    def _():
-        product(x, a, x_cols, cols, *args)
-
-    store_parts(acc, far, near, 0)
-
-
-def first_kernel(tile, slots, col_tiles, cols, x_cols, y_cols, scaling, a, x, y, far, near, table, scaled, acc):
-    core = lax.axis_index("slab") % 2
-    hub = (core + lax.axis_index("blk")) % 2
-    emit = accumulate(acc, tile)
+    product(a, a, cols, cols, scaling, table, scaled, tile, slots, col_tiles, emit)
+    give[:rows, :] = acc[y_lo]
+    keep[:rows, :] = acc[y_lo]
+    give[rows:, :] = acc[1 - y_lo, pl.ds(pl.multiple_of((1 - core) * tile, tile), tile), :]
+    keep[rows:, :] = acc[1 - y_lo, pl.ds(pl.multiple_of(core * tile, tile), tile), :]
+
+
+def fetch(copies, sems):
+    started = [pltpu.make_async_copy(src, dst, sems.at[n]) for n, (src, dst) in enumerate(copies)]
+    for copy in started:
+        copy.start()
+    return started
+
+
+def other_kernel(tile, slots, col_tiles, cols, x_cols, y_cols, scaling, a_any, x_any, y_any, p1, p2, p3, kept2,
+                 q1, q2, q3, kept1, a, x, y, table, scaled, acc, sems):
+    slab = lax.axis_index("slab")
+    core = slab % 2
+    hub = (core + lax.axis_index("blk")) % 2 == 1
+    rows = a.shape[0]
+    half = tile // 2
+    copies = fetch([(a_any, a), (x_any, x)], sems)
+    third = pltpu.make_async_copy(y_any, y, sems.at[2])
+
+    @pl.when(hub)
+    def _():
+        third.start()
+
+    def emit(i, b, value):
+        at = pl.ds(pl.multiple_of(i * tile, tile), tile)
+        acc[2 * b, at, :] += value[:, :half]
+        acc[2 * b + 1, at, :] += value[:, half:]
+
     args = (scaling, table, scaled, tile, slots, col_tiles, emit)
     acc[...] = jnp.zeros_like(acc)
-
-    @pl.when((hub == 1) & (core == 0))
-    def _():
-        product(y, x, y_cols, x_cols, *args)
-
-    @pl.when((hub == 1) & (core == 1))
-    def _():
-        product(y, a, y_cols, cols, *args)
-
-    store_parts(acc, far, near, 0)
-    acc[...] = jnp.zeros_like(acc)
-
-    @pl.when((hub == 1) & (core == 0))
-    def _():
-        product(a, y, cols, y_cols, *args)
-
-    @pl.when((hub == 1) & (core == 1))
-    def _():
-        product(x, y, x_cols, y_cols, *args)
-
-    store_parts(acc, far, near, acc.shape[1])
-
-
-def combine_kernel(near2, got2, near1, got1, cross, ahead, first0, first1, kept):
+    for copy in copies:
+        copy.wait()
+
+    @pl.when(core == 0)
+    def _():
+        product(a, x, cols, x_cols, *args)
+
+    @pl.when(core == 1)
+    def _():
+        product(x, a, x_cols, cols, *args)
+
+    kept2[...] = acc[slab]
+    for k, ref in ((1, p1), (2, p2), (3, p3)):
+        ref[...] = acc[slab ^ k].astype(ref.dtype)
+
+    def store(start):
+        kept1[start:start + rows, :] = acc[slab]
+        for k, ref in ((1, q1), (2, q2), (3, q3)):
+            ref[start:start + rows, :] = acc[slab ^ k].astype(ref.dtype)
+
+    @pl.when(jnp.logical_not(hub))
+    def _():
+        kept1[...] = jnp.zeros_like(kept1)
+
+    @pl.when(hub)
+    def _():
+        acc[...] = jnp.zeros_like(acc)
+        third.wait()
+
+        @pl.when(core == 0)
+        def _():
+            product(y, x, y_cols, x_cols, *args)
+
+        @pl.when(core == 1)
+        def _():
+            product(y, a, y_cols, cols, *args)
+
+        store(0)
+        acc[...] = jnp.zeros_like(acc)
+
+        @pl.when(core == 0)
+        def _():
+            product(a, y, cols, y_cols, *args)
+
+        @pl.when(core == 1)
+        def _():
+            product(x, y, x_cols, y_cols, *args)
+
+        store(rows)
+
+
+def combine_kernel(k2, r1, r2, r3, k1, t1, t2, t3, ahead, beside, own2, own1, v2, u1, u2, u3, v1, w1, w2, w3, sems):
     core = lax.axis_index("slab") % 2
-    rows, width = near2.shape
-    half = width // 2
-    plane2 = near2[...] + got2[...].astype(jnp.float32)
-    plane1 = near1[rows:, :] + got1[rows:, :].astype(jnp.float32)
-    other1 = near1[:rows, :] + got1[:rows, :].astype(jnp.float32)
-    first0[...] = other1[:, :half].astype(jnp.bfloat16)
-    first1[...] = other1[:, half:].astype(jnp.bfloat16)
-    for start, value in ((0, plane2), (rows, plane1)):
-        mine = jnp.where(core == 0, value[:, :half], value[:, half:])
-        theirs = jnp.where(core == 0, value[:, half:], value[:, :half])
-        cross[start:start + rows, :] = theirs.astype(jnp.bfloat16)
-        ahead[start:start + rows, :] = mine.astype(jnp.bfloat16)
-        kept[start:start + rows, :] = mine
+    pairs = [(k2, v2), (r1, u1), (r2, u2), (r3, u3), (k1, v1), (t1, w1), (t2, w2), (t3, w3)]
+    copies = fetch(pairs, sems)
+    rows = k2.shape[0]
+    wide = lambda ref: ref[...].astype(jnp.float32)
+    for copy in copies[:4]:
+        copy.wait()
+    same = v2[...] + wide(u2)
+    swapped = wide(u1) + wide(u3)
+    own2[...] = jnp.where(core == 0, same, swapped)
+    ahead[:rows, :] = jnp.where(core == 0, swapped, same).astype(ahead.dtype)
+    for copy in copies[4:]:
+        copy.wait()
+    plane1 = v1[...] + wide(w1) + wide(w2) + wide(w3)
+    beside[...] = plane1[:rows].astype(beside.dtype)
+    ahead[rows:, :] = plane1[rows:].astype(ahead.dtype)
+    own1[...] = plane1[rows:]
 
 
 def eliminate(matrix, size, group):
@@ -220,7 +241,7 @@
                 precision=HIGH, preferred_element_type=jnp.float32)
 
 
-def panel_kernel(tile, panel, part, other, column, lower, total, w, u):
+def panel_kernel(tile, panel, keep, got, mine, theirs, column, lower, total, w, u):
     slab = lax.axis_index("slab")
     core = slab % 2
     y_lo = slab // 2
@@ -228,7 +249,10 @@
     block = panel[0]
     pos = block % 2
     holds = (block // 2 == lax.axis_index("blk")) & (pos == y_lo)
-    total[...] = part[...] + other[...]
+    rows = total.shape[0]
+    total[...] = keep[:rows, :] + got[:rows, :]
+    total[pl.ds(pl.multiple_of(core * tile, tile), tile), :] += mine[...]
+    total[pl.ds(pl.multiple_of((1 - core) * tile, tile), tile), :] += theirs[...]
     eye = jnp.where(
         lax.broadcasted_iota(jnp.int32, (tile, tile), 0) == lax.broadcasted_iota(jnp.int32, (tile, tile), 1),
         jnp.float32(ridge_shift), jnp.float32(0.0))
@@ -260,13 +284,12 @@
         column[other_rows, :] = u[rows, tile:].T
 
 
-def final_kernel(tile, panel, column, lower, kept, cross, ahead, first0, first1, out):
+def final_kernel(tile, panel, column, lower, own2, own1, ahead, beside, out):
     slab = lax.axis_index("slab")
     core = slab % 2
     y_lo = slab // 2
     half = tile // 2
     group = lax.axis_index("blk")
-    odd = group % 2
     rows = column.shape[0]
     block = panel[0]
     pos = block % 2
@@ -280,31 +303,9 @@
         out[0, here, :] = out[0, here, :] - lax.dot_general(
             left, right, (((0,), (0,)), ((), ())), precision=HIGH, preferred_element_type=jnp.float32)
 
-    wide = lambda ref, start: ref[start:start + rows, :].astype(jnp.float32)
-
-    @pl.when(core == 0)
-    def _():
-        out[2] = kept[:rows, :] + wide(cross, 0)
-
-        @pl.when(odd == 1)
-        def _():
-            out[1] = kept[rows:, :] + wide(first0, 0)
-
-        @pl.when(odd == 0)
-        def _():
-            out[1] = wide(cross, rows) + wide(first0, 0)
-
-    @pl.when(core == 1)
-    def _():
-        out[2] = wide(ahead, 0) + wide(cross, 0)
-
-        @pl.when(odd == 1)
-        def _():
-            out[1] = wide(cross, rows) + wide(first1, 0)
-
-        @pl.when(odd == 0)
-        def _():
-            out[1] = wide(ahead, rows) + wide(first1, 0)
+    out[2] = own2[...] + ahead[:rows, :].astype(jnp.float32)
+    late = jnp.where(group % 2 == 1, own1[...], ahead[rows:, :].astype(jnp.float32))
+    out[1] = late + beside[...].astype(jnp.float32)
 
 
 def make_body(groups, slabs):
@@ -314,13 +315,9 @@
     hubs = [(g, s) for g, s in devices if (g + s) % 2 == 1]
     far_pairs = [(at(g, s), at(g + (2 if forward(s) else -2), s)) for g, s in devices]
     near_pairs = [(at(g + (-1 if forward(s) else 1), s), at(g, s)) for g, s in hubs]
-    chip_pairs = [(at(g, s), at(g, s ^ 2)) for g, s in devices]
-    chip_hub_pairs = [(at(g, s), at(g, s ^ 2)) for g, s in hubs]
-    core_pairs = [(at(g, s), at(g, s ^ 1)) for g, s in devices]
-    cross_pairs = [(at(g, s), at(g, s + 1) if forward(s) else at(g + 2, s - 1)) for g, s in devices]
-    ahead_pairs = [(at(g, s), at(g + 2, s)) for g, s in devices if not forward(s)]
-    first0_pairs = [(at(g, s), at(g - 1, s) if forward(s) else at(g + 1, s - 1)) for g, s in hubs]
-    first1_pairs = [(at(g, s), at(g - 1, s + 1) if forward(s) else at(g + 1, s)) for g, s in hubs]
+    slab_pairs = lambda k, among=devices: [(at(g, s), at(g, s ^ k)) for g, s in among]
+    ahead_pairs = [(at(g, s), at(g + 2, s)) for g, s in devices]
+    beside_pairs = [(at(g, s), at(g ^ 1, s)) for g, s in devices]
 
     def move(value, pairs):
         return lax.ppermute(value, AXES, pairs)
@@ -344,53 +341,56 @@
         y_cols = move(cols, near_pairs)
         table = pltpu.SMEM((2, col_tiles + 1), jnp.int32)
         scaled = pltpu.VMEM((tile, tile), bf16)
-        acc = pltpu.VMEM((2, rows, tile), f32)
         sizes = (tile, slots, col_tiles)
-        far0, near0 = pl.pallas_call(
+        give, keep = pl.pallas_call(
             lambda *refs: own_kernel(*sizes, *refs),
-            out_shape=(shape((rows, tile), f32), shape((rows, tile), f32)),
+            out_shape=(shape((rows + tile, tile), f32), shape((rows + tile, tile), f32)),
             in_specs=[SMEM, VMEM, VMEM], out_specs=(VMEM, VMEM),
-            scratch_shapes=[table, scaled], name="plane_zero",
+            scratch_shapes=[table, scaled, pltpu.VMEM((2, rows, tile), f32)], name="plane_zero",
         )(cols, scales, a_tiles)
-        part = near0 + move(far0, chip_pairs)
-        other = move(part, core_pairs)
+        got = move(give, slab_pairs(1))
+        mine = move(keep[rows:] + got[rows:], slab_pairs(2))
+        x, y, mine = lax.optimization_barrier((x, y, mine))
+        part = shape((rows, half), bf16)
+        two = shape((2 * rows, half), bf16)
+        p1, p2, p3, kept2, q1, q2, q3, kept1 = pl.pallas_call(
+            lambda *refs: other_kernel(*sizes, *refs),
+            out_shape=(part, part, part, shape((rows, half), f32), two, two, two, shape((2 * rows, half), f32)),
+            in_specs=[SMEM, SMEM, SMEM, VMEM, ANY, ANY, ANY], out_specs=(VMEM,) * 8,
+            scratch_shapes=[pltpu.VMEM(a_tiles.shape, bf16)] * 3 + [
+                table, scaled, pltpu.VMEM((4, rows, half), f32), pltpu.SemaphoreType.DMA((3,))],
+            name="planes_one_two",
+        )(cols, x_cols, y_cols, scales, a_tiles, x, y)
+        r2, t2 = move(p2, slab_pairs(2)), move(q2, slab_pairs(2, hubs))
+        r3, t3 = move(p3, slab_pairs(3)), move(q3, slab_pairs(3, hubs))
+        r1, t1 = move(p1, slab_pairs(1)), move(q1, slab_pairs(1, hubs))
+        mine, kept2 = lax.optimization_barrier((mine, kept2))
+        theirs = move(mine, slab_pairs(1))
+        theirs, kept2 = lax.optimization_barrier((theirs, kept2))
         column, lower = pl.pallas_call(
             lambda *refs: panel_kernel(tile, *refs),
             out_shape=(shape((rows, half), f32), shape((tile, tile), bf16)),
-            in_specs=[SMEM, VMEM, VMEM], out_specs=(VMEM, VMEM),
+            in_specs=[SMEM] + [VMEM] * 4, out_specs=(VMEM, VMEM),
             scratch_shapes=[pltpu.VMEM((rows, tile), f32), pltpu.VMEM((tile, rows), f32), pltpu.VMEM((tile, rows), f32)],
             name="panel_step",
-        )(panel, part, other)
-        lower = move(lower, chip_pairs)
-        far2, near2 = pl.pallas_call(
-            lambda *refs: second_kernel(*sizes, *refs),
-            out_shape=(shape((rows, tile), bf16), shape((rows, tile), f32)),
-            in_specs=[SMEM, SMEM, VMEM, VMEM, VMEM], out_specs=(VMEM, VMEM),
-            scratch_shapes=[table, scaled, acc], name="plane_two",
-        )(cols, x_cols, scales, a_tiles, x)
-        got2 = move(far2, chip_pairs)
-        far1, near1 = pl.pallas_call(
-            lambda *refs: first_kernel(*sizes, *refs),
-            out_shape=(shape((2 * rows, tile), bf16), shape((2 * rows, tile), f32)),
-            in_specs=[SMEM, SMEM, SMEM, VMEM, VMEM, VMEM, VMEM], out_specs=(VMEM, VMEM),
-            scratch_shapes=[table, scaled, acc], name="plane_one",
-        )(cols, x_cols, y_cols, scales, a_tiles, x, y)
-        got1 = move(far1, chip_hub_pairs)
-        cross, ahead, first0, first1, kept = pl.pallas_call(
+        )(panel, keep, got, mine, theirs)
+        kept2, lower = lax.optimization_barrier((kept2, lower))
+        lower = move(lower, slab_pairs(2))
+        parts = (kept2, r1, r2, r3, kept1, t1, t2, t3)
+        ahead, beside, own2, own1 = pl.pallas_call(
             combine_kernel,
-            out_shape=(shape((2 * rows, half), bf16), shape((2 * rows, half), bf16), shape((rows, half), bf16),
-                       shape((rows, half), bf16), shape((2 * rows, half), f32)),
-            in_specs=[VMEM] * 4, out_specs=(VMEM,) * 5, name="combine",
-        )(near2, got2, near1, got1)
-        cross = move(cross, cross_pairs)
+            out_shape=(two, part, shape((rows, half), f32), shape((rows, half), f32)),
+            in_specs=[ANY] * 8, out_specs=(VMEM,) * 4,
+            scratch_shapes=[pltpu.VMEM(v.shape, v.dtype) for v in parts] + [pltpu.SemaphoreType.DMA((8,))],
+            name="combine",
+        )(*parts)
+        beside = move(beside, beside_pairs)
         ahead = move(ahead, ahead_pairs)
-        first0 = move(first0, first0_pairs)
-        first1 = move(first1, first1_pairs)
         out = pl.pallas_call(
             lambda *refs: final_kernel(tile, *refs),
             out_shape=shape((3, rows, half), f32),
-            in_specs=[SMEM] + [VMEM] * 7, out_specs=VMEM, name="assemble",
-        )(panel, column, lower, kept, cross, ahead, first0, first1)
+            in_specs=[SMEM] + [VMEM] * 6, out_specs=VMEM, name="assemble",
+        )(panel, column, lower, own2, own1, ahead, beside)
         return out.transpose(1, 0, 2)
 
     return body

time: 105 us -> 88.8 us (0.85)
  the two profiles are of different devices: /device:TPU:161 before, /device:TPU:1 now
where the time goes in v2:
time: 88.8 us; the launch traced here: 90.5 us
  starting transfers between devices  33.1 us (37%)
  waiting for transfers between devices  28.4 us (32%)
  Pallas kernels  22.1 us (25%)
  local copies, waits for them, and re-layouts  3.52 us (4%)
  other arithmetic  2.49 us (3%)
  between operations  0.89 us (1%)
    ppermute x16, starting transfers between devices, move(): return lax.ppermute(value, AXES, pairs)  33.1 us
    ppermute x16, waiting for transfers between devices, move(): return lax.ppermute(value, AXES, pairs)  28.4 us
    pallas_call x1, Pallas kernels, body(): pl.pallas_call(lambda *refs: other_kernel(*sizes, *refs), out_shape=(part...  8.3 us
    pallas_call x1, Pallas kernels, body(): pl.pallas_call(lambda *refs: own_kernel(*sizes, *refs), out_shape=(shape(...  6.36 us
    pallas_call x1, Pallas kernels, body(): pl.pallas_call(lambda *refs: panel_kernel(tile, *refs), out_shape=(shape(...  2.6 us
    pallas_call x1, Pallas kernels, body(): pl.pallas_call(combine_kernel, out_shape=(two, part, shape((rows, half),...  2.57 us
    pallas_call x1, Pallas kernels, body(): pl.pallas_call(lambda *refs: final_kernel(tile, *refs), out_shape=shape((...  2.24 us
    unnamed x32, local copies, waits for them, and re-layouts  2.19 us
  transfers between devices with their start and end apart: 16, of which 6 were waited for; matrix products, arithmetic and copies ran while one was open for 4% of the time, Pallas kernels for 10%

profile of v2, /device:TPU:1, one launch (start us, length us, event | category | flops | bytes accessed | tf_op | source)
XLA Modules:
  0.0 90.5 jit_solution(14199560290133885460)
XLA Ops:
  0.0 8.6 %collective-permute-start.1 = (bf16[512,2048]{1,0:T(8,128)(2,1)}, bf16[512,2048]{1,0:T(8,128)(2,1)S(1)}, u32[]{:S(2)}, u32[]{:S(2)}) collective-permute-start(bf16[512,2048]{1,0:T(8,128)(2,1)} %refs_4_.1), channel_id=1, source_target_pairs={{0,8},{1,249},{2,10},{3,251},{4,12},{5,253},{6,14},{7,255},{8,16},... | collective-permute-start | bytes 6291464 | tf_op jit(solution)/shard_map/ppermute | solution.py:323
  8.6 1.3 %collective-permute-start.2 = (bf16[512,2048]{1,0:T(8,128)(2,1)}, bf16[512,2048]{1,0:T(8,128)(2,1)}, u32[]{:S(2)}, u32[]{:S(2)}) collective-permute-start(bf16[512,2048]{1,0:T(8,128)(2,1)} %refs_4_.1), channel_id=1, source_target_pairs={{5,1},{7,3},{0,4},{2,6},{13,9},{15,11},{8,12},{10,14},{21,17},{23,... | collective-permute-start | bytes 6291464 | tf_op jit(solution)/shard_map/ppermute | solution.py:323
  9.9 1.3 %reshape.3.refs_1_.refs_3_ = f32[16,256]{1,0:T(8,128)} reshape(f32[4096]{0:T(1024)} %param.8) | data formatting | bytes 32768 | tf_op jit(solution)/shard_map/reshape | solution.py:337
  11.2 1.3 %compare_select_fusion.refs_0_ = s32[2,8]{1,0:T(2,128)} fusion(s32[2,8]{1,0:T(2,128)} %bitcast.3, s32[2]{0:T(128)} %bitcast.4), kind=kLoop, calls=%fused_computation.1 | loop fusion | flops 32 | bytes 136 | tf_op jit(solution)/shard_map/jit(_where)/select_n | solution.py:336
  12.6 6.4 %plane_zero.1 = (f32[768,256]{1,0:T(8,128)}, f32[768,256]{1,0:T(8,128)}) custom-call(s32[2,8]{1,0:T(2,128)} %compare_select_fusion.refs_0_, f32[16,256]{1,0:T(8,128)} %reshape.3.refs_1_.refs_3_, bf16[512,2048]{1,0:T(8,128)(2,1)} %refs_4_.1), custom_call_target="tpu_custom_call" | custom-call | tf_op jit(solution)/shard_map/plane_zero/pallas_call | solution.py:345
  18.9 2.5 %collective-permute-done.refs_2_ = f32[768,256]{1,0:T(8,128)S(1)} collective-permute-done((f32[768,256]{1,0:T(8,128)}, f32[768,256]{1,0:T(8,128)S(1)}, u32[]{:S(2)}, u32[]{:S(2)}) %collective-permute-start) | collective-permute-done | bytes 786464 | tf_op jit(solution)/shard_map/ppermute | solution.py:323
  21.4 1.1 %slice_add_fusion = f32[256,256]{1,0:T(8,128)S(1)} fusion(f32[768,256]{1,0:T(8,128)S(1)} %collective-permute-done.refs_2_, f32[768,256]{1,0:T(8,128)} %get-tuple-element.30.refs_1_), kind=kLoop, calls=%fused_computation | loop fusion | flops 65536 | bytes 786432 | tf_op jit(solution)/shard_map/add | solution.py:352
  22.6 1.7 %collective-permute-start.3 = (f32[256,256]{1,0:T(8,128)S(1)}, f32[256,256]{1,0:T(8,128)S(1)}, u32[]{:S(2)}, u32[]{:S(2)}) collective-permute-start(f32[256,256]{1,0:T(8,128)S(1)} %slice_add_fusion), channel_id=1, source_target_pairs={{0,2},{1,3},{2,0},{3,1},{4,6},{5,7},{6,4},{7,5},{8,10},{9,11},{10,... | collective-permute-start | bytes 786440 | tf_op jit(solution)/shard_map/ppermute | solution.py:323
  24.2 6.9 %collective-permute-start.4 = (s32[2,8]{1,0:T(2,128)S(1)}, s32[2,8]{1,0:T(2,128)S(1)}, u32[]{:S(2)}, u32[]{:S(2)}) collective-permute-start(s32[2,8]{1,0:T(2,128)S(1)} %copy-done.13), channel_id=1, source_target_pairs={{0,8},{1,249},{2,10},{3,251},{4,12},{5,253},{6,14},{7,255},{8,16},... | collective-permute-start | bytes 200 | tf_op jit(solution)/shard_map/ppermute | solution.py:323
  31.1 1.3 %collective-permute-start.5 = (s32[2,8]{1,0:T(2,128)S(1)}, s32[2,8]{1,0:T(2,128)S(1)}, u32[]{:S(2)}, u32[]{:S(2)}) collective-permute-start(s32[2,8]{1,0:T(2,128)S(1)} %copy-done.13), channel_id=1, source_target_pairs={{5,1},{7,3},{0,4},{2,6},{13,9},{15,11},{8,12},{10,14},{21,17},{23,... | collective-permute-start | bytes 200 | tf_op jit(solution)/shard_map/ppermute | solution.py:323
  32.4 7.6 %collective-permute-done.2.refs_6_ = bf16[512,2048]{1,0:T(8,128)(2,1)} collective-permute-done((bf16[512,2048]{1,0:T(8,128)(2,1)}, bf16[512,2048]{1,0:T(8,128)(2,1)}, u32[]{:S(2)}, u32[]{:S(2)}) %collective-permute-start.2) | collective-permute-done | bytes 2097184 | tf_op jit(solution)/shard_map/ppermute | solution.py:323
  40.0 2.7 %collective-permute-done.5.refs_2_ = s32[2,8]{1,0:T(2,128)S(1)} collective-permute-done((s32[2,8]{1,0:T(2,128)S(1)}, s32[2,8]{1,0:T(2,128)S(1)}, u32[]{:S(2)}, u32[]{:S(2)}) %collective-permute-start.5) | collective-permute-done | bytes 96 | tf_op jit(solution)/shard_map/ppermute | solution.py:323
  43.3 8.3 %planes_one_two.1 = (bf16[512,128]{1,0:T(8,128)(2,1)}, bf16[512,128]{1,0:T(8,128)(2,1)}, bf16[512,128]{1,0:T(8,128)(2,1)}, f32[512,128]{1,0:T(8,128)}, bf16[1024...) custom-call(s32[2,8]{1,0:T(2,128)} %compare_select_fusion.refs_0_, ...), custom_call_target="tpu_custom_call" | custom-call | tf_op jit(solution)/shard_map/planes_one_two/pallas_call | solution.py:356
  51.7 6.1 %collective-permute-start.10 = (bf16[512,128]{1,0:T(8,128)(2,1)}, bf16[512,128]{1,0:T(8,128)(2,1)S(1)}, u32[]{:S(2)}, u32[]{:S(2)}) collective-permute-start(bf16[512,128]{1,0:T(8,128)(2,1)} %get-tuple-element.46), channel_id=1, source_target_pairs={{0,3},{1,2},{2,1},{3,0},{4,7},{5,6},{6,5},{7,4},{8,11},{9,10},{10,... | collective-permute-start | bytes 393224 | tf_op jit(solution)/shard_map/ppermute | solution.py:323
  57.9 2.0 %collective-permute-start.11 = (bf16[1024,128]{1,0:T(8,128)(2,1)}, bf16[1024,128]{1,0:T(8,128)(2,1)S(1)}, u32[]{:S(2)}, u32[]{:S(2)}) collective-permute-start(bf16[1024,128]{1,0:T(8,128)(2,1)} %get-tuple-element.48), channel_id=1, source_target_pairs={{1,0},{3,2},{4,5},{6,7},{9,8},{11,10},{12,13},{14,15},{17,16},{19,... | collective-permute-start | bytes 786440 | tf_op jit(solution)/shard_map/ppermute | solution.py:323
  59.9 1.9 %collective-permute-start.12 = (bf16[1024,128]{1,0:T(8,128)(2,1)}, bf16[1024,128]{1,0:T(8,128)(2,1)S(1)}, u32[]{:S(2)}, u32[]{:S(2)}) collective-permute-start(bf16[1024,128]{1,0:T(8,128)(2,1)} %get-tuple-element.49), channel_id=1, source_target_pairs={{1,3},{3,1},{4,6},{6,4},{9,11},{11,9},{12,14},{14,12},{17,19},{19,... | collective-permute-start | bytes 786440 | tf_op jit(solution)/shard_map/ppermute | solution.py:323
  61.8 1.3 %collective-permute-start.13 = (bf16[1024,128]{1,0:T(8,128)(2,1)}, bf16[1024,128]{1,0:T(8,128)(2,1)S(1)}, u32[]{:S(2)}, u32[]{:S(2)}) collective-permute-start(bf16[1024,128]{1,0:T(8,128)(2,1)} %get-tuple-element.50), channel_id=1, source_target_pairs={{1,2},{3,0},{4,7},{6,5},{9,10},{11,8},{12,15},{14,13},{17,18},{19,... | collective-permute-start | bytes 786440 | tf_op jit(solution)/shard_map/ppermute | solution.py:323
  63.3 1.5 %collective-permute-start.9 = (bf16[512,128]{1,0:T(8,128)(2,1)}, bf16[512,128]{1,0:T(8,128)(2,1)S(1)}, u32[]{:S(2)}, u32[]{:S(2)}) collective-permute-start(bf16[512,128]{1,0:T(8,128)(2,1)} %get-tuple-element.45), channel_id=1, source_target_pairs={{0,2},{1,3},{2,0},{3,1},{4,6},{5,7},{6,4},{7,5},{8,10},{9,11},{10,... | collective-permute-start | bytes 393224 | tf_op jit(solution)/shard_map/ppermute | solution.py:323
  65.5 2.6 %panel_step.1 = (f32[512,128]{1,0:T(8,128)}, bf16[256,256]{1,0:T(8,128)(2,1)}) custom-call(s32[1]{0:T(128)S(6)} %copy.6.refs_0_, f32[768,256]{1,0:T(8,128)} %get-tuple-element.30.refs_1_, f32[768,256]{1,0:T(8,128)} %copy-done.1, f32[256,256]{1,0:T(8,128)} %copy-done.2, f32[256,256]{1,0:T(8,128)} %copy-done.6), custom_call_target="tpu_custom_call" | custom-call | tf_op jit(solution)/shard_map/panel_step/pallas_call | solution.py:370
  68.1 4.7 %collective-permute-done.9.r2 = bf16[512,128]{1,0:T(8,128)(2,1)S(1)} collective-permute-done((bf16[512,128]{1,0:T(8,128)(2,1)}, bf16[512,128]{1,0:T(8,128)(2,1)S(1)}, u32[]{:S(2)}, u32[]{:S(2)}) %collective-permute-start.9) | collective-permute-done | bytes 131104 | tf_op jit(solution)/shard_map/ppermute | solution.py:323
  73.7 2.6 %combine.1 = (bf16[1024,128]{1,0:T(8,128)(2,1)}, bf16[512,128]{1,0:T(8,128)(2,1)}, f32[512,128]{1,0:T(8,128)}, f32[512,128]{1,0:T(8,128)}) custom-call(f32[512,128]{1,0:T(8,128)} %get-tuple-element.43.k2, bf16[512,128]{1,0:T(8,128)(2,1)} %copy-done.11, bf16[512,128]{1,0:T(8,128)(2,1)} %copy-done.12, bf16[512,128]{1,0:T(8,128)(2,1)} %copy-done.10, ...), custom_call_target="tpu_custom_call" | custom-call | tf_op jit(solution)/shard_map/combine/pallas_call | solution.py:380
  76.6 7.0 %collective-permute-done.15.refs_6_ = bf16[512,128]{1,0:T(8,128)(2,1)S(1)} collective-permute-done((bf16[512,128]{1,0:T(8,128)(2,1)}, bf16[512,128]{1,0:T(8,128)(2,1)S(1)}, u32[]{:S(2)}, u32[]{:S(2)}) %collective-permute-start.15) | collective-permute-done | bytes 131104 | tf_op jit(solution)/shard_map/ppermute | solution.py:323
  83.7 3.8 %collective-permute-done.14.refs_5_ = bf16[1024,128]{1,0:T(8,128)(2,1)S(1)} collective-permute-done((bf16[1024,128]{1,0:T(8,128)(2,1)}, bf16[1024,128]{1,0:T(8,128)(2,1)S(1)}, u32[]{:S(2)}, u32[]{:S(2)}) %collective-permute-start.14) | collective-permute-done | bytes 262176 | tf_op jit(solution)/shard_map/ppermute | solution.py:323
  88.2 2.2 %assemble.1 = f32[3,512,128]{2,1,0:T(8,128)} custom-call(s32[1]{0:T(128)S(6)} %copy.6.refs_0_, f32[512,128]{1,0:T(8,128)} %get-tuple-element.39.refs_1_, bf16[256,256]{1,0:T(8,128)(2,1)} %copy-done.9, f32[512,128]{1,0:T(8,128)} %get-tuple-element.51.refs_3_, f32[512,128]{1,0:T(8,128)} %get-tuple-element.52.refs_4_, bf16[1024,128]{1,0:T(8,128)(2,1)} %copy-done.7, ...), custom_call_target="tpu_custom_call" | custom-call | tf_op jit(solution)/shard_map/assemble/pallas_call | solution.py:389
  (48 shorter events, 2.7 us)
Async XLA Ops:
  0.0 32.4 %collective-permute-start.1 = (bf16[512,2048]{1,0:T(8,128)(2,1)}, bf16[512,2048]{1,0:T(8,128)(2,1)S(1)}, u32[]{:S(2)}, u32[]{:S(2)}) collective-permute-start(bf16[512,2048]{1,0:T(8,128)(2,1)} %refs_4_.1), channel_id=1, source_target_pairs={{0,8},{1,249},{2,10},{3,251},{4,12},{5,253},{6,14},{7,255},{8,16},... | collective-permute-start | bytes 6291464 | tf_op jit(solution)/shard_map/ppermute | solution.py:323
  8.6 31.4 %collective-permute-start.2 = (bf16[512,2048]{1,0:T(8,128)(2,1)}, bf16[512,2048]{1,0:T(8,128)(2,1)}, u32[]{:S(2)}, u32[]{:S(2)}) collective-permute-start(bf16[512,2048]{1,0:T(8,128)(2,1)} %refs_4_.1), channel_id=1, source_target_pairs={{5,1},{7,3},{0,4},{2,6},{13,9},{15,11},{8,12},{10,14},{21,17},{23,... | collective-permute-start | bytes 6291464 | tf_op jit(solution)/shard_map/ppermute | solution.py:323
  12.6 11.7 %copy-start.13 = (s32[2,8]{1,0:T(2,128)S(1)}, s32[2,8]{1,0:T(2,128)}, u32[]{:S(2)}) copy-start(s32[2,8]{1,0:T(2,128)} %compare_select_fusion.refs_0_) | copy-start | bytes 196
  18.9 2.5 %collective-permute-start = (f32[768,256]{1,0:T(8,128)}, f32[768,256]{1,0:T(8,128)S(1)}, u32[]{:S(2)}, u32[]{:S(2)}) collective-permute-start(f32[768,256]{1,0:T(8,128)} %get-tuple-element.31), channel_id=1, source_target_pairs={{0,1},{1,0},{2,3},{3,2},{4,5},{5,4},{6,7},{7,6},{8,9},{9,8},{10,11... | collective-permute-start | bytes 2359304 | tf_op jit(solution)/shard_map/ppermute | solution.py:323
  21.4 30.2 %copy-start.1 = (f32[768,256]{1,0:T(8,128)}, f32[768,256]{1,0:T(8,128)S(1)}, u32[]{:S(2)}) copy-start(f32[768,256]{1,0:T(8,128)S(1)} %collective-permute-done.refs_2_) | copy-start | bytes 2359300
  22.6 9.8 %collective-permute-start.3 = (f32[256,256]{1,0:T(8,128)S(1)}, f32[256,256]{1,0:T(8,128)S(1)}, u32[]{:S(2)}, u32[]{:S(2)}) collective-permute-start(f32[256,256]{1,0:T(8,128)S(1)} %slice_add_fusion), channel_id=1, source_target_pairs={{0,2},{1,3},{2,0},{3,1},{4,6},{5,7},{6,4},{7,5},{8,10},{9,11},{10,... | collective-permute-start | bytes 786440 | tf_op jit(solution)/shard_map/ppermute | solution.py:323
  24.2 15.8 %collective-permute-start.4 = (s32[2,8]{1,0:T(2,128)S(1)}, s32[2,8]{1,0:T(2,128)S(1)}, u32[]{:S(2)}, u32[]{:S(2)}) collective-permute-start(s32[2,8]{1,0:T(2,128)S(1)} %copy-done.13), channel_id=1, source_target_pairs={{0,8},{1,249},{2,10},{3,251},{4,12},{5,253},{6,14},{7,255},{8,16},... | collective-permute-start | bytes 200 | tf_op jit(solution)/shard_map/ppermute | solution.py:323
  31.1 11.6 %collective-permute-start.5 = (s32[2,8]{1,0:T(2,128)S(1)}, s32[2,8]{1,0:T(2,128)S(1)}, u32[]{:S(2)}, u32[]{:S(2)}) collective-permute-start(s32[2,8]{1,0:T(2,128)S(1)} %copy-done.13), channel_id=1, source_target_pairs={{5,1},{7,3},{0,4},{2,6},{13,9},{15,11},{8,12},{10,14},{21,17},{23,... | collective-permute-start | bytes 200 | tf_op jit(solution)/shard_map/ppermute | solution.py:323
  32.4 33.1 %copy-start.2 = (f32[256,256]{1,0:T(8,128)}, f32[256,256]{1,0:T(8,128)S(1)}, u32[]{:S(2)}) copy-start(f32[256,256]{1,0:T(8,128)S(1)} %collective-permute-done.3.refs_3_) | copy-start | bytes 786436
  32.4 10.3 %copy-start = (bf16[512,2048]{1,0:T(8,128)(2,1)}, bf16[512,2048]{1,0:T(8,128)(2,1)S(1)}, u32[]{:S(2)}) copy-start(bf16[512,2048]{1,0:T(8,128)(2,1)S(1)} %collective-permute-done.1.refs_5_) | copy-start | bytes 6291460
  51.6 11.6 %collective-permute-start.6 = (f32[256,256]{1,0:T(8,128)S(1)}, f32[256,256]{1,0:T(8,128)S(1)}, u32[]{:S(2)}, u32[]{:S(2)}) collective-permute-start(f32[256,256]{1,0:T(8,128)S(1)} %collective-permute-done.3.refs_3_), channel_id=1, source_target_pairs={{0,1},{1,0},{2,3},{3,2},{4,5},{5,4},{6,7},{7,6},{8,9},{9,8},{10,11... | collective-permute-start | bytes 786440 | tf_op jit(solution)/shard_map/ppermute | solution.py:323
  51.7 11.4 %collective-permute-start.10 = (bf16[512,128]{1,0:T(8,128)(2,1)}, bf16[512,128]{1,0:T(8,128)(2,1)S(1)}, u32[]{:S(2)}, u32[]{:S(2)}) collective-permute-start(bf16[512,128]{1,0:T(8,128)(2,1)} %get-tuple-element.46), channel_id=1, source_target_pairs={{0,3},{1,2},{2,1},{3,0},{4,7},{5,6},{6,5},{7,4},{8,11},{9,10},{10,... | collective-permute-start | bytes 393224 | tf_op jit(solution)/shard_map/ppermute | solution.py:323
  57.9 15.0 %collective-permute-start.11 = (bf16[1024,128]{1,0:T(8,128)(2,1)}, bf16[1024,128]{1,0:T(8,128)(2,1)S(1)}, u32[]{:S(2)}, u32[]{:S(2)}) collective-permute-start(bf16[1024,128]{1,0:T(8,128)(2,1)} %get-tuple-element.48), channel_id=1, source_target_pairs={{1,0},{3,2},{4,5},{6,7},{9,8},{11,10},{12,13},{14,15},{17,16},{19,... | collective-permute-start | bytes 786440 | tf_op jit(solution)/shard_map/ppermute | solution.py:323
  59.9 13.0 %collective-permute-start.12 = (bf16[1024,128]{1,0:T(8,128)(2,1)}, bf16[1024,128]{1,0:T(8,128)(2,1)S(1)}, u32[]{:S(2)}, u32[]{:S(2)}) collective-permute-start(bf16[1024,128]{1,0:T(8,128)(2,1)} %get-tuple-element.49), channel_id=1, source_target_pairs={{1,3},{3,1},{4,6},{6,4},{9,11},{11,9},{12,14},{14,12},{17,19},{19,... | collective-permute-start | bytes 786440 | tf_op jit(solution)/shard_map/ppermute | solution.py:323
  61.8 11.0 %collective-permute-start.13 = (bf16[1024,128]{1,0:T(8,128)(2,1)}, bf16[1024,128]{1,0:T(8,128)(2,1)S(1)}, u32[]{:S(2)}, u32[]{:S(2)}) collective-permute-start(bf16[1024,128]{1,0:T(8,128)(2,1)} %get-tuple-element.50), channel_id=1, source_target_pairs={{1,2},{3,0},{4,7},{6,5},{9,10},{11,8},{12,15},{14,13},{17,18},{19,... | collective-permute-start | bytes 786440 | tf_op jit(solution)/shard_map/ppermute | solution.py:323
  63.1 9.7 %copy-start.10 = (bf16[512,128]{1,0:T(8,128)(2,1)}, bf16[512,128]{1,0:T(8,128)(2,1)S(1)}, u32[]{:S(2)}) copy-start(bf16[512,128]{1,0:T(8,128)(2,1)S(1)} %collective-permute-done.10.r3) | copy-start | bytes 393220
  63.1 4.9 %collective-permute-start.8 = (bf16[512,128]{1,0:T(8,128)(2,1)}, bf16[512,128]{1,0:T(8,128)(2,1)S(1)}, u32[]{:S(2)}, u32[]{:S(2)}) collective-permute-start(bf16[512,128]{1,0:T(8,128)(2,1)} %get-tuple-element.44), channel_id=1, source_target_pairs={{0,1},{1,0},{2,3},{3,2},{4,5},{5,4},{6,7},{7,6},{8,9},{9,8},{10,11... | collective-permute-start | bytes 393224 | tf_op jit(solution)/shard_map/ppermute | solution.py:323
  63.3 9.6 %collective-permute-start.9 = (bf16[512,128]{1,0:T(8,128)(2,1)}, bf16[512,128]{1,0:T(8,128)(2,1)S(1)}, u32[]{:S(2)}, u32[]{:S(2)}) collective-permute-start(bf16[512,128]{1,0:T(8,128)(2,1)} %get-tuple-element.45), channel_id=1, source_target_pairs={{0,2},{1,3},{2,0},{3,1},{4,6},{5,7},{6,4},{7,5},{8,10},{9,11},{10,... | collective-permute-start | bytes 393224 | tf_op jit(solution)/shard_map/ppermute | solution.py:323
  68.1 4.8 %copy-start.11 = (bf16[512,128]{1,0:T(8,128)(2,1)}, bf16[512,128]{1,0:T(8,128)(2,1)S(1)}, u32[]{:S(2)}) copy-start(bf16[512,128]{1,0:T(8,128)(2,1)S(1)} %collective-permute-done.8.r1) | copy-start | bytes 393220
  76.3 11.2 %collective-permute-start.14 = (bf16[1024,128]{1,0:T(8,128)(2,1)}, bf16[1024,128]{1,0:T(8,128)(2,1)S(1)}, u32[]{:S(2)}, u32[]{:S(2)}) collective-permute-start(bf16[1024,128]{1,0:T(8,128)(2,1)} %get-tuple-element.53), channel_id=1, source_target_pairs={{0,8},{1,9},{2,10},{3,11},{4,12},{5,13},{6,14},{7,15},{8,16},{9,17... | collective-permute-start | bytes 786440 | tf_op jit(solution)/shard_map/ppermute | solution.py:323
  76.4 7.2 %collective-permute-start.15 = (bf16[512,128]{1,0:T(8,128)(2,1)}, bf16[512,128]{1,0:T(8,128)(2,1)S(1)}, u32[]{:S(2)}, u32[]{:S(2)}) collective-permute-start(bf16[512,128]{1,0:T(8,128)(2,1)} %get-tuple-element.54), channel_id=1, source_target_pairs={{0,4},{1,5},{2,6},{3,7},{4,0},{5,1},{6,2},{7,3},{8,12},{9,13},{10,... | collective-permute-start | bytes 393224 | tf_op jit(solution)/shard_map/ppermute | solution.py:323
  76.5 7.1 %collective-permute-start.7 = (bf16[256,256]{1,0:T(8,128)(2,1)}, bf16[256,256]{1,0:T(8,128)(2,1)S(1)}, u32[]{:S(2)}, u32[]{:S(2)}) collective-permute-start(bf16[256,256]{1,0:T(8,128)(2,1)} %get-tuple-element.42), channel_id=1, source_target_pairs={{0,2},{1,3},{2,0},{3,1},{4,6},{5,7},{6,4},{7,5},{8,10},{9,11},{10,... | collective-permute-start | bytes 393224 | tf_op jit(solution)/shard_map/ppermute | solution.py:323
  83.6 3.8 %copy-start.8 = (bf16[512,128]{1,0:T(8,128)(2,1)}, bf16[512,128]{1,0:T(8,128)(2,1)S(1)}, u32[]{:S(2)}) copy-start(bf16[512,128]{1,0:T(8,128)(2,1)S(1)} %collective-permute-done.15.refs_6_) | copy-start | bytes 393220
  83.6 3.8 %copy-start.9 = (bf16[256,256]{1,0:T(8,128)(2,1)}, bf16[256,256]{1,0:T(8,128)(2,1)S(1)}, u32[]{:S(2)}) copy-start(bf16[256,256]{1,0:T(8,128)(2,1)S(1)} %collective-permute-done.7.refs_2_) | copy-start | bytes 393220
  (8 other events, 9.3 us)
